TPU v7x, 32 devices: a whole 2x2x4 slice. The times are simulated.
32 devices in a mesh: dp: 2 (over x), sp: 4 (over y, core), ctx: 4 (over z).
Axes of the slice: x: 2, y: 2, z: 4, core: 2. Of those that a mesh axis runs over, the one named last changes fastest.
Arguments:
- tokens: bfloat16 [2, 2048, 768], P('dp', ('sp', 'ctx')), may hold values from -6 to 6
- cotangent: bfloat16 [2, 2048, 768], P('dp', ('sp', 'ctx')), may hold values from -6 to 6
- lengths: int32 [2], P('dp'), may hold values from 512 to 2048, as said below
- kept_keys: int32 [2, 4, 512, 12, 64], P('dp', None, 'ctx', 'sp'), may hold values from 0 to 1983, as said below
- first_gain: bfloat16 [768], P('dp'), may hold values from 0.5 to 1.5
- qkv_weight: bfloat16 [768, 2304], P('dp'), may hold values from -0.21875 to 0.21875
- score_weight: bfloat16 [768, 12], P('dp'), may hold values from -0.4375 to 0.4375
- out_weight: bfloat16 [768, 768], P('dp'), may hold values from -1.25 to 1.25
- second_gain: bfloat16 [768], P('dp'), may hold values from 0.5 to 1.5
- fc_weight: bfloat16 [768, 3072], P('dp'), may hold values from -0.21875 to 0.21875
- proj_weight: bfloat16 [3072, 768], P('dp'), may hold values from -0.15625 to 0.15625
Outputs:
- output: bfloat16 [2, 2048, 768], P('dp', ('sp', 'ctx'))
- input_grad: bfloat16 [2, 2048, 768], P('dp', ('sp', 'ctx'))
- first_gain_grad: float32 [768], P('dp')
- qkv_grad: float32 [768, 2304], P('dp')
- score_grad: float32 [768, 12], P('dp')
- out_grad: float32 [768, 768], P('dp')
- second_gain_grad: float32 [768], P('dp')
- fc_grad: float32 [768, 3072], P('dp')
- proj_grad: float32 [3072, 768], P('dp')
Inputs may be any that keep to these rules, and one draw needn't show every extreme that they name: `lengths`: the valid tokens of a slot stand at its start; in every draw some slot is full. `kept_keys`: an entry for the query at position t names a key position of the same slot at most t - 64; where t < 64 the entries are 0 and unused. Positions may repeat.
All inputs are finite; a program needn't handle non-finite values.
Results may differ from a plain program's by a relative error of at most 0.02.
Values may be sent and summed in bfloat16 or wider, within the bound.
No kernel may reach another device: no remote copies, remote signals or barrier semaphores. Data moves between devices by JAX's collectives and lax.ppermute only.
A program may use at most 256 MiB of HBM per device.

v0:
```python
import jax
import jax.numpy as jnp
from jax import lax
from jax.sharding import PartitionSpec as P

H = 12
HD = 64
WIN = 64
SLOT = 2048


EPSILON = 1e-05


def layer_norm(values, gain):
    mean_value = jnp.mean(values, axis=-1, keepdims=True)
    centred = values - mean_value
    variance = jnp.mean(centred * centred, axis=-1, keepdims=True)
    return centred * lax.rsqrt(variance + EPSILON) * gain


def tanh_gelu(values):
    return jax.nn.gelu(values, approximate=True)


def contract_rows(left, right):
    return lax.dot_general(
        left, right, (((0,), (0,)), ((), ())), preferred_element_type=jnp.float32
    )


def contract_cols(left, right):
    return lax.dot_general(
        left, right, (((1,), (1,)), ((), ())), preferred_element_type=jnp.float32
    )


def slab_rows(gathered, first_pos, row_count):
    span_len = row_count + WIN
    return jax.vmap(lambda offset: lax.dynamic_slice_in_dim(gathered, offset, span_len, 0))(
        first_pos
    )


def tile_scores(queries, first_pos, picked, pairs_full, gates_full):
    group_count, row_count, head_count, head_width = queries.shape
    score_scale = head_width ** (-0.5)
    pair_slab = slab_rows(pairs_full, first_pos, row_count)
    key_slab = pair_slab[..., :head_width]
    value_slab = pair_slab[..., head_width:]
    gate_slab = slab_rows(gates_full, first_pos, row_count)
    head_ids = jnp.arange(head_count, dtype=jnp.int32)[None, None, :, None]
    rows_at = picked + WIN
    pair_pick = pairs_full[rows_at, head_ids]
    key_pick = pair_pick[..., :head_width]
    value_pick = pair_pick[..., head_width:]
    near_scores = (
        jnp.einsum("grhd,gjhd->grhj", queries, key_slab, preferred_element_type=jnp.float32)
        * score_scale
    )
    near_scores = near_scores + jnp.swapaxes(gate_slab, 1, 2)[:, None]
    far_scores = (
        jnp.einsum("grhd,grhmd->grhm", queries, key_pick, preferred_element_type=jnp.float32)
        * score_scale
    )
    far_scores = far_scores + gates_full[rows_at, head_ids]
    row_ids = jnp.arange(row_count, dtype=jnp.int32)[None, :, None, None]
    col_ids = jnp.arange(row_count + WIN, dtype=jnp.int32)[None, None, None, :]
    start_pos = first_pos[:, None, None, None]
    near_ok = (col_ids > row_ids) & (col_ids <= row_ids + WIN) & (col_ids + start_pos >= WIN)
    far_ok = jnp.broadcast_to(start_pos + row_ids >= WIN, far_scores.shape)
    scores = jnp.concatenate(
        [jnp.where(near_ok, near_scores, -1e30), jnp.where(far_ok, far_scores, -1e30)], axis=-1
    )
    return (scores, key_slab, value_slab, key_pick, value_pick, rows_at, head_ids)


def tile_of(array, tile_index, group_count, row_count, row_tiles):
    starts = (tile_index // row_tiles * group_count, tile_index % row_tiles * row_count) + (0,) * (
        array.ndim - 2
    )
    return array


def stitch(blocks, group_tiles, row_tiles):
    shape = blocks.shape
    grid = blocks.reshape((group_tiles, row_tiles) + shape[1:])
    grid = jnp.swapaxes(grid, 1, 2)
    return grid.reshape((group_tiles * shape[1], row_tiles * shape[2]) + shape[3:])


def per_device(
    tokens,
    cotangent,
    lengths,
    kept_keys,
    first_gain,
    qkv_weight,
    score_weight,
    out_weight,
    second_gain,
    fc_weight,
    proj_weight,
):
    gathered = (
        lax.all_gather(first_gain, "dp", axis=0, tiled=True),
        lax.all_gather(qkv_weight, "dp", axis=0, tiled=True),
        lax.all_gather(score_weight, "dp", axis=0, tiled=True),
        lax.all_gather(out_weight, "dp", axis=0, tiled=True),
        lax.all_gather(second_gain, "dp", axis=0, tiled=True),
        lax.all_gather(fc_weight, "dp", axis=0, tiled=True),
        lax.all_gather(proj_weight, "dp", axis=0, tiled=True),
    )
    gain_one, qkv_full, score_full, out_full, gain_two, fc_full, proj_full = gathered
    gain_one = gain_one.astype(jnp.float32)
    gain_two = gain_two.astype(jnp.float32)
    seg_count = lax.axis_size("sp")
    ctx_count = lax.axis_size("ctx")
    local_rows = tokens.shape[1]
    heads_here = H // seg_count
    segment = SLOT // seg_count
    ctx_at = lax.axis_index("ctx")
    positions = (lax.axis_index("sp") * ctx_count + ctx_at) * local_rows + jnp.arange(
        local_rows, dtype=jnp.int32
    )
    is_valid = positions < lengths[0]
    inputs = tokens[0].astype(jnp.float32)
    norm_one = layer_norm(inputs, gain_one).astype(jnp.bfloat16)
    qkv_rows = jnp.dot(norm_one, qkv_full, preferred_element_type=jnp.float32).astype(jnp.bfloat16)
    key_score = jnp.dot(norm_one, score_full, preferred_element_type=jnp.float32).astype(
        jnp.bfloat16
    )
    head_qkv, head_score = (
        lax.all_to_all(qkv_rows, "sp", split_axis=1, concat_axis=0, tiled=True),
        lax.all_to_all(key_score, "sp", split_axis=1, concat_axis=0, tiled=True),
    )
    triple = head_qkv.reshape(seg_count, local_rows, heads_here, 3 * HD)
    queries = triple[..., :HD]
    pairs = triple[..., HD:].reshape(seg_count, local_rows, heads_here * 2 * HD)
    local_scores = head_score.reshape(seg_count, local_rows, heads_here)
    all_pairs, all_scores = (
        lax.all_gather(pairs, "ctx", axis=1, tiled=True),
        lax.all_gather(local_scores, "ctx", axis=1, tiled=True),
    )
    pair_full = all_pairs.reshape(SLOT, heads_here, 2 * HD)
    pairs_full = jnp.pad(pair_full, ((WIN, 0), (0, 0), (0, 0)))
    raw_scores = all_scores.reshape(SLOT, heads_here).astype(jnp.float32)
    gate_plain = -jnp.log1p(jnp.exp(-raw_scores))
    gates_full = jnp.pad(gate_plain, ((WIN, 0), (0, 0)))
    picked_local = kept_keys[0]
    group_start = jnp.arange(seg_count, dtype=jnp.int32) * segment + ctx_at * local_rows
    row_count = min(512, local_rows)
    group_count = min(seg_count, max(1, 512 // local_rows))
    row_tiles = local_rows // row_count
    group_tiles = seg_count // group_count
    tile_total = group_tiles * row_tiles
    span_len = row_count + WIN
    score_scale = HD ** (-0.5)

    def tile_first(tile_index):
        return group_start + tile_index % row_tiles * row_count

    def forward_tile(tile_index):
        first_pos = tile_first(tile_index)
        query_tile = tile_of(queries, tile_index, group_count, row_count, row_tiles)
        picked = tile_of(picked_local, tile_index, group_count, row_count, row_tiles)
        scores, _, value_slab, _, value_pick, _, _ = tile_scores(
            query_tile, first_pos, picked, pairs_full, gates_full
        )
        largest = jnp.max(scores, axis=-1, keepdims=True)
        expo = jnp.exp(scores - largest)
        denominator = jnp.sum(expo, axis=-1, keepdims=True)
        weights = (expo / denominator).astype(jnp.bfloat16)
        near_out = jnp.einsum(
            "grhj,gjhd->grhd",
            weights[..., :span_len],
            value_slab,
            preferred_element_type=jnp.float32,
        )
        far_out = jnp.einsum(
            "grhm,grhmd->grhd",
            weights[..., span_len:],
            value_pick,
            preferred_element_type=jnp.float32,
        )
        return (near_out + far_out, (largest + jnp.log(denominator))[..., 0])

    tile_outs, tile_logs = lax.map(forward_tile, jnp.arange(tile_total, dtype=jnp.int32))
    attended_heads = stitch(tile_outs, group_tiles, row_tiles).astype(jnp.bfloat16)
    log_totals = stitch(tile_logs, group_tiles, row_tiles)
    attended = lax.all_to_all(
        attended_heads.reshape(seg_count * local_rows, heads_here * HD),
        "sp",
        split_axis=0,
        concat_axis=1,
        tiled=True,
    )
    mixed = inputs + jnp.dot(attended, out_full, preferred_element_type=jnp.float32)
    norm_two = layer_norm(mixed, gain_two).astype(jnp.bfloat16)
    hidden_pre = jnp.dot(norm_two, fc_full, preferred_element_type=jnp.float32)
    active = tanh_gelu(hidden_pre).astype(jnp.bfloat16)
    result = jnp.where(
        is_valid[:, None],
        mixed + jnp.dot(active, proj_full, preferred_element_type=jnp.float32),
        0.0,
    )
    output = result.astype(jnp.bfloat16)[None]
    grad_out = jnp.where(is_valid[:, None], cotangent[0], jnp.zeros_like(cotangent[0]))
    proj_grad = contract_rows(active, grad_out)
    grad_active = contract_cols(grad_out, proj_full)
    _, gelu_pull = jax.vjp(tanh_gelu, hidden_pre)
    grad_pre = gelu_pull(grad_active)[0].astype(jnp.bfloat16)
    fc_grad = contract_rows(norm_two, grad_pre)
    grad_norm_two = contract_cols(grad_pre, fc_full)
    _, second_pull = jax.vjp(layer_norm, mixed, gain_two)
    grad_mixed_norm, second_gain_grad = second_pull(grad_norm_two)
    grad_mixed = grad_out.astype(jnp.float32) + grad_mixed_norm
    grad_branch = grad_mixed.astype(jnp.bfloat16)
    out_grad = contract_rows(attended, grad_branch)
    grad_attended = contract_cols(grad_branch, out_full).astype(jnp.bfloat16)
    head_grad = lax.all_to_all(grad_attended, "sp", split_axis=1, concat_axis=0, tiled=True)
    grad_grid = head_grad.reshape(seg_count, local_rows, heads_here, HD)

    def backward_tile(carry, tile_index):
        key_grad, value_grad, gate_grad = carry
        first_pos = tile_first(tile_index)
        query_tile = tile_of(queries, tile_index, group_count, row_count, row_tiles)
        picked = tile_of(picked_local, tile_index, group_count, row_count, row_tiles)
        grad_tile = tile_of(grad_grid, tile_index, group_count, row_count, row_tiles)
        log_tile = tile_of(log_totals, tile_index, group_count, row_count, row_tiles)
        scores, key_slab, value_slab, key_pick, value_pick, rows_at, head_ids = tile_scores(
            query_tile, first_pos, picked, pairs_full, gates_full
        )
        prob = jnp.exp(scores - log_tile[..., None])
        weights = prob.astype(jnp.bfloat16)
        grad_prob = jnp.concatenate(
            [
                jnp.einsum(
                    "grhd,gjhd->grhj", grad_tile, value_slab, preferred_element_type=jnp.float32
                ),
                jnp.einsum(
                    "grhd,grhmd->grhm", grad_tile, value_pick, preferred_element_type=jnp.float32
                ),
            ],
            axis=-1,
        )
        row_dot = jnp.sum(prob * grad_prob, axis=-1, keepdims=True)
        grad_scores = (prob * (grad_prob - row_dot)).astype(jnp.bfloat16)
        near_grad = grad_scores[..., :span_len]
        far_grad = grad_scores[..., span_len:]
        far_weights = weights[..., span_len:]
        grad_query = (
            jnp.einsum("grhj,gjhd->grhd", near_grad, key_slab, preferred_element_type=jnp.float32)
            + jnp.einsum("grhm,grhmd->grhd", far_grad, key_pick, preferred_element_type=jnp.float32)
        ) * score_scale
        rows_here = first_pos[:, None] + jnp.arange(span_len, dtype=jnp.int32)[None, :]
        key_grad = key_grad.at[rows_here].add(
            jnp.einsum("grhj,grhd->gjhd", near_grad, query_tile, preferred_element_type=jnp.float32)
            * score_scale
        )
        value_grad = value_grad.at[rows_here].add(
            jnp.einsum(
                "grhj,grhd->gjhd",
                weights[..., :span_len],
                grad_tile,
                preferred_element_type=jnp.float32,
            )
        )
        gate_grad = gate_grad.at[rows_here].add(
            jnp.swapaxes(jnp.sum(near_grad.astype(jnp.float32), axis=1), 1, 2)
        )
        key_grad = key_grad.at[rows_at, head_ids].add(
            jnp.einsum("grhm,grhd->grhmd", far_grad, query_tile, preferred_element_type=jnp.float32)
            * score_scale
        )
        value_grad = value_grad.at[rows_at, head_ids].add(
            jnp.einsum(
                "grhm,grhd->grhmd", far_weights, grad_tile, preferred_element_type=jnp.float32
            )
        )
        gate_grad = gate_grad.at[rows_at, head_ids].add(far_grad.astype(jnp.float32))
        return ((key_grad, value_grad, gate_grad), grad_query)

    zero_keys = jnp.zeros((SLOT + WIN, heads_here, HD), jnp.float32)
    zero_gates = jnp.zeros((SLOT + WIN, heads_here), jnp.float32)
    (key_grad, value_grad, gate_grad), query_tiles = lax.scan(
        backward_tile, (zero_keys, zero_keys, zero_gates), jnp.arange(tile_total, dtype=jnp.int32)
    )
    grad_queries = stitch(query_tiles, group_tiles, row_tiles)
    pair_grad = jnp.concatenate([key_grad[WIN:], value_grad[WIN:]], axis=-1).reshape(
        seg_count, segment, heads_here * 2 * HD
    )
    gate_total = gate_grad[WIN:].reshape(seg_count, segment, heads_here)
    pair_mine, gate_mine = (
        lax.psum_scatter(pair_grad, "ctx", scatter_dimension=1, tiled=True),
        lax.psum_scatter(gate_total, "ctx", scatter_dimension=1, tiled=True),
    )
    score_here = local_scores.astype(jnp.float32)
    grad_key_score = (gate_mine * jax.nn.sigmoid(-score_here)).astype(jnp.bfloat16)
    grad_triple = jnp.concatenate(
        [grad_queries, pair_mine.reshape(seg_count, local_rows, heads_here, 2 * HD)], axis=-1
    )
    grad_triple = grad_triple.astype(jnp.bfloat16).reshape(
        seg_count * local_rows, heads_here * 3 * HD
    )
    grad_qkv, grad_score = (
        lax.all_to_all(grad_triple, "sp", split_axis=0, concat_axis=1, tiled=True),
        lax.all_to_all(
            grad_key_score.reshape(seg_count * local_rows, heads_here),
            "sp",
            split_axis=0,
            concat_axis=1,
            tiled=True,
        ),
    )
    qkv_grad = contract_rows(norm_one, grad_qkv)
    score_grad = contract_rows(norm_one, grad_score)
    grad_norm_one = contract_cols(grad_qkv, qkv_full) + contract_cols(grad_score, score_full)
    _, first_pull = jax.vjp(layer_norm, inputs, gain_one)
    grad_input_norm, first_gain_grad = first_pull(grad_norm_one)
    input_grad = (grad_mixed + grad_input_norm).astype(jnp.bfloat16)[None]
    shards = (
        lax.psum_scatter(
            first_gain_grad.astype(jnp.bfloat16), "dp", scatter_dimension=0, tiled=True
        ).astype(jnp.float32),
        lax.psum_scatter(
            qkv_grad.astype(jnp.bfloat16), "dp", scatter_dimension=0, tiled=True
        ).astype(jnp.float32),
        lax.psum_scatter(
            score_grad.astype(jnp.bfloat16), "dp", scatter_dimension=0, tiled=True
        ).astype(jnp.float32),
        lax.psum_scatter(
            out_grad.astype(jnp.bfloat16), "dp", scatter_dimension=0, tiled=True
        ).astype(jnp.float32),
        lax.psum_scatter(
            second_gain_grad.astype(jnp.bfloat16), "dp", scatter_dimension=0, tiled=True
        ).astype(jnp.float32),
        lax.psum_scatter(
            fc_grad.astype(jnp.bfloat16), "dp", scatter_dimension=0, tiled=True
        ).astype(jnp.float32),
        lax.psum_scatter(
            proj_grad.astype(jnp.bfloat16), "dp", scatter_dimension=0, tiled=True
        ).astype(jnp.float32),
    )
    reduced = (
        lax.psum(shards[0].astype(jnp.bfloat16), ("sp", "ctx")).astype(jnp.float32),
        lax.psum(shards[1].astype(jnp.bfloat16), ("sp", "ctx")).astype(jnp.float32),
        lax.psum(shards[2].astype(jnp.bfloat16), ("sp", "ctx")).astype(jnp.float32),
        lax.psum(shards[3].astype(jnp.bfloat16), ("sp", "ctx")).astype(jnp.float32),
        lax.psum(shards[4].astype(jnp.bfloat16), ("sp", "ctx")).astype(jnp.float32),
        lax.psum(shards[5].astype(jnp.bfloat16), ("sp", "ctx")).astype(jnp.float32),
        lax.psum(shards[6].astype(jnp.bfloat16), ("sp", "ctx")).astype(jnp.float32),
    )
    return (
        output,
        input_grad,
        reduced[0],
        reduced[1],
        reduced[2],
        reduced[3],
        reduced[4],
        reduced[5],
        reduced[6],
    )


def solution(mesh):
    placed = (
        P("dp", ("sp", "ctx"), None),
        P("dp", ("sp", "ctx"), None),
        P("dp"),
        P("dp", None, "ctx", "sp", None),
        P("dp"),
        P("dp", None),
        P("dp", None),
        P("dp", None),
        P("dp"),
        P("dp", None),
        P("dp", None),
    )
    return jax.shard_map(
        per_device,
        mesh=mesh,
        in_specs=placed,
        out_specs=(
            P("dp", ("sp", "ctx"), None),
            P("dp", ("sp", "ctx"), None),
            P("dp"),
            P("dp", None),
            P("dp", None),
            P("dp", None),
            P("dp"),
            P("dp", None),
            P("dp", None),
        ),
        check_vma=False,
    )
```

profile of v0, /device:TPU:0, one launch (start us, length us, event | category | flops | bytes accessed | tf_op | source)
XLA Modules:
  0.0 4547.1 jit_solution(11578294361857887183)
XLA Ops:
  13.7 47.9 %all-gather.8.cloned.1.call-done = bf16[768,2304]{1,0:T(8,128)(2,1)} async-done(((bf16[384,2304]{1,0:T(8,128)(2,1)}), bf16[768,2304]{1,0:T(8,128)(2,1)}) %all-gather.8.cloned.1.call-update) | async-done | bytes 3538960 | tf_op jit(solution)/shard_map/all_gather | solution.py:107
  64.6 12.1 all_to_all.96
  99.0 11.5 all_gather.31
  110.6 7.6 while.1
  118.3 845.3 %gather_fusion.2 = f32[98304]{0:T(1024)S(1)} fusion(f32[2112,3]{0,1:T(4,128)S(1)} %get-tuple-element.181, s32[98304]{0:T(1024)S(1)} %reshape.446), kind=kCustom, calls=%fused_computation.2 | custom fusion | bytes 1572864 | tf_op jit(solution)/shard_map/while/body/eval_jaxpr/gather | solution.py:66
  985.2 939.6 %gather_fusion.1 = bf16[98304,128]{1,0:T(8,128)(2,1)} fusion(bf16[2112,3,128]{2,0,1:T(8,128)(2,1)S(1)} %copy.158, s32[98304]{0:T(1024)S(1)} %reshape.446), kind=kCustom, calls=%fused_computation.1 | custom fusion | bytes 51118080 | tf_op jit(solution)/shard_map/while/body/eval_jaxpr/gather | solution.py:54
  1924.8 18.5 multiply_reduce_fusion.3
  1949.5 25.1 multiply_reduce_fusion.2
  2015.1 23.8 multiply_reduce_fusion.1
  2047.6 78.2 %scatter_fusion.1 = f32[2112,3,64]{2,1,0:T(4,128)} fusion(f32[2112,3,64]{2,1,0:T(4,128)} %broadcast_in_dim.202.clone, s32[768]{0:T(1024)S(1)} %reshape.460, f32[768,3,64]{2,1,0:T(4,128)S(1)} %bitcast.194), kind=kCustom, calls=%fused_computation.4 | custom fusion | flops 147456 | bytes 1772544 | tf_op jit(solution)/shard_map/while/body/eval_jaxpr/scatter-add | solution.py:261
  2125.8 6.0 reshape.411
  2136.4 78.2 %scatter_fusion = f32[2112,3,64]{2,1,0:T(4,128)} fusion(f32[2112,3,64]{2,1,0:T(4,128)} %broadcast_in_dim.202.clone.1, s32[768]{0:T(1024)S(1)} %reshape.460, f32[768,3,64]{2,1,0:T(4,128)S(1)} %bitcast.195), kind=kCustom, calls=%fused_computation.3 | custom fusion | flops 147456 | bytes 1772544 | tf_op jit(solution)/shard_map/while/body/eval_jaxpr/scatter-add | solution.py:257
  2219.1 27.7 multiply_reduce_fusion
  2246.7 540.7 %scatter_fusion.2 = f32[6336,64]{1,0:T(8,128)S(1)} fusion(f32[6336,64]{1,0:T(8,128)S(1)} %reshape.407, s32[98304]{0:T(1024)} %reshape.482, f32[98304,64]{1,0:T(8,128)} %bitcast.187), kind=kCustom, calls=%fused_computation.6 | custom fusion | flops 6291456 | bytes 75890688
  2789.3 5.8 reshape.430
  2795.1 18.4 broadcast_multiply_fusion
  2813.5 540.9 %scatter_fusion.3 = f32[6336,64]{1,0:T(8,128)S(1)} fusion(f32[6336,64]{1,0:T(8,128)S(1)} %copy-done, s32[98304]{0:T(1024)} %reshape.482, f32[98304,64]{1,0:T(8,128)} %bitcast.188), kind=kCustom, calls=%fused_computation.7 | custom fusion | flops 6291456 | bytes 75890688
  3362.1 5.9 pad_maximum_fusion
  3372.6 46.1 %copy.205 = f32[4,512,384]{0,2,1:T(8,128)} copy(f32[4,512,384]{2,1,0:T(8,128)S(1)} %reshape.517) | data formatting | bytes 6291456
  3418.7 89.4 %reshape.518 = f32[512,1536]{1,0:T(8,128)} reshape(f32[512,384,4]{2,1,0:T(8,128)} %bitcast.51) | data formatting | bytes 6291456
  3513.2 6.4 scatter_custom_fusion.2
  3520.1 621.1 %scatter_fusion.4 = f32[6336]{0:T(1024)S(1)} fusion(f32[6336]{0:T(1024)S(1)} %reshape.415, s32[98304]{0:T(1024)S(1)} %reshape.494, f32[98304]{0:T(1024)S(1)} %reshape.496), kind=kCustom, calls=%fused_computation.8 | custom fusion | flops 98304 | bytes 1572864
  4157.9 29.1 reshape.519
  4187.0 12.1 copy.171
  4199.2 11.9 all_to_all.97
  4215.4 6.1 all_to_all.98
  4223.0 22.7 reduce-scatter.20.cloned.1.call-done
  4245.8 62.8 %reduce-scatter.18.cloned.1.call-done = bf16[384,3072]{1,0:T(8,128)(2,1)} async-done(((bf16[768,3072]{1,0:T(8,128)(2,1)}), bf16[384,3072]{1,0:T(8,128)(2,1)}) %reduce-scatter.18.cloned.1.call-update) | async-done | bytes 2359312 | tf_op jit(solution)/shard_map/reduce_scatter | solution.py:338
  4308.6 50.6 %reduce-scatter.14.cloned.1.call-done = bf16[384,2304]{1,0:T(8,128)(2,1)} async-done(((bf16[768,2304]{1,0:T(8,128)(2,1)}), bf16[384,2304]{1,0:T(8,128)(2,1)}) %reduce-scatter.14.cloned.1.call-update) | async-done | bytes 1769488 | tf_op jit(solution)/shard_map/reduce_scatter | solution.py:326
  4365.1 7.8 reduce-scatter.26.cloned.1.call-done
  4382.9 63.7 %all-reduce.6 = (bf16[384]{0:T(512)(128)(2,1)S(1)}, bf16[384,12]{0,1:T(8,128)(2,1)S(1)}, bf16[384]{0:T(512)(128)(2,1)S(1)}) all-reduce(bf16[384]{0:T(512)(128)(2,1)S(1)} %dynamic-slice.5, bf16[384,12]{0,1:T(8,128)(2,1)S(1)} %copy.210, bf16[384]{0:T(512)(128)(2,1)S(1)} %dynamic-slice.7), channel_id=1, replica_groups=mesh['dp'=2,'sp'=4,'ctx'=4] {'sp','ctx'}, use_global_device_ids=true, to_apply=%region_23.24 | all-reduce | flops 5376 | bytes 21504 | tf_op jit(solution)/shard_map/psum | solution.py:346
  4449.3 80.6 %all-reduce.11.cloned.1.call-done = (bf16[384,2304]{1,0:T(8,128)(2,1)}, bf16[384,768]{1,0:T(8,128)(2,1)}, bf16[384,3072]{1,0:T(8,128)(2,1)}, bf16[1536,768]{1,0:T(8,128)(2,1)}) async-done(((bf16[384,2304]{1,0:T(8,128)(2,1)}, bf16[384,768]{1,0:T(8,128)(2,1)}, bf16[384,3072]{1,0:T(8,128)(2,1)}, bf16[1536,768]{1,0:T(8,128)(2,1)}), (bf16[384,2304]{1,0:T(8,128)(2,1)}, bf16[384,768]{1,0:T(8,128)(2,1)}, ...) | async-done | bytes 7077904 | tf_op jit(solution)/shard_map/psum | solution.py:347
  (361 shorter events, 194.1 us)
Async XLA Ops:
  7.2 54.4 %all-gather.8.cloned.1.call-start = ((), (), s32[]{:S(2)}) async-start(), calls=%async_computation.13 | async-start | bytes 5308416 | tf_op jit(solution)/shard_map/all_gather | solution.py:107
  7.9 958.5 %all-gather.10.cloned.1.call-start = ((), (), s32[]{:S(2)}) async-start(), calls=%async_computation.14 | async-start | bytes 1966080 | tf_op jit(solution)/shard_map/all_gather | solution.py:142
  13.3 71.2 %copy-start.45 = (f32[768]{0:T(1024)}, f32[768]{0:T(1024)S(1)}, u32[]{:S(2)}) copy-start(f32[768]{0:T(1024)S(1)} %reshape.507) | copy-start | bytes 9220
  13.5 71.0 %copy-start.53 = (f32[128]{0:T(128)}, f32[128]{0:T(128)S(1)}, u32[]{:S(2)}) copy-start(f32[128]{0:T(128)S(1)} %broadcast_multiply_fusion.2) | copy-start | bytes 1540
  13.7 48.0 %copy-start.73 = (f32[128]{0:T(128)}, f32[128]{0:T(128)S(1)}, u32[]{:S(2)}) copy-start(f32[128]{0:T(128)S(1)} %fusion.41) | copy-start | bytes 1540
  13.7 70.8 %copy-start.63 = (f32[128]{0:T(128)}, f32[128]{0:T(128)S(1)}, u32[]{:S(2)}) copy-start(f32[128]{0:T(128)S(1)} %fusion.53) | copy-start | bytes 1540
  78.6 1906.4 %all-gather.12.cloned.1.call-start = ((), (), s32[]{:S(2)}) async-start(), calls=%async_computation.15 | async-start | bytes 1769472 | tf_op jit(solution)/shard_map/all_gather | solution.py:109
  79.4 1909.6 %all-gather.14.cloned.1.call-start = ((), (), s32[]{:S(2)}) async-start(), calls=%async_computation.16 | async-start | bytes 7077888 | tf_op jit(solution)/shard_map/all_gather | solution.py:111
  85.4 13.5 all-to-all-start.1
  88.7 1903.5 %all-gather.16.cloned.1.call-start = ((), (), s32[]{:S(2)}) async-start(), calls=%async_computation.17 | async-start | bytes 7077888 | tf_op jit(solution)/shard_map/all_gather | solution.py:112
  99.0 19.3 copy-start.51
  966.4 958.4 %copy-start.11 = (f32[4,128,3,64]{3,2,1,0:T(4,128)}, f32[4,128,3,64]{3,2,1,0:T(4,128)S(1)}, u32[]{:S(2)}) copy-start(f32[4,128,3,64]{3,2,1,0:T(4,128)S(1)} %copy.219) | copy-start | bytes 1179652
  985.2 958.4 %copy-start.38 = (bf16[4,192,3,64]{1,3,2,0:T(8,128)(2,1)}, bf16[4,192,3,64]{1,3,2,0:T(8,128)(2,1)S(1)}, u32[]{:S(2)}) copy-start(bf16[4,192,3,64]{1,3,2,0:T(8,128)(2,1)S(1)} %copy.218) | copy-start | bytes 884740
  1924.8 18.8 copy-start.47
  1924.8 18.8 copy-start.81
  1946.8 29.4 copy-start.17
  1977.2 9.2 all-to-all-start.2
  1981.8 17.7 copy-start.43
  1981.9 154.5 %copy-start.50 = (s32[768]{0:T(1024)}, s32[768]{0:T(1024)S(1)}, u32[]{:S(2)}) copy-start(s32[768]{0:T(1024)S(1)} %reshape.460) | copy-start | bytes 9220
  2002.2 8.6 all-to-all-start.3
  2005.6 2152.3 %reduce-scatter.22.cloned.1.call-start = ((), (), s32[]{:S(2)}) async-start(), calls=%async_computation.22 | async-start | bytes 3932160
  2015.1 23.8 copy-start.12
  2795.1 18.4 copy-start
  3508.1 706.2 %reduce-scatter.24.cloned.1.call-start = ((), (), s32[]{:S(2)}) async-start(), calls=%async_computation.23 | async-start | bytes 327680
  4143.0 80.0 %reduce-scatter.16.cloned.1.call-start = ((), (), s32[]{:S(2)}) async-start(), calls=%async_computation.19 | async-start | bytes 1769472 | tf_op jit(solution)/shard_map/reduce_scatter | solution.py:332
  4144.6 101.1 %reduce-scatter.20.cloned.1.call-start = ((), (), s32[]{:S(2)}) async-start(), calls=%async_computation.21 | async-start | bytes 7077888 | tf_op jit(solution)/shard_map/reduce_scatter | solution.py:341
  4148.6 160.0 %reduce-scatter.18.cloned.1.call-start = ((), (), s32[]{:S(2)}) async-start(), calls=%async_computation.20 | async-start | bytes 7077888 | tf_op jit(solution)/shard_map/reduce_scatter | solution.py:338
  4153.5 205.6 %reduce-scatter.14.cloned.1.call-start = ((), (), s32[]{:S(2)}) async-start(), calls=%async_computation.18 | async-start | bytes 5308416 | tf_op jit(solution)/shard_map/reduce_scatter | solution.py:326
  4214.2 158.7 %reduce-scatter.26.cloned.1.call-start = ((), (), s32[]{:S(2)}) async-start(), calls=%async_computation.24 | async-start | bytes 294912
  4222.7 307.2 %all-reduce.11.cloned.1.call-start = ((), (), s32[]{:S(2)}) async-start(), calls=%async_computation.25 | async-start | bytes 14155776 | tf_op jit(solution)/shard_map/psum | solution.py:347
  4377.2 71.2 %copy-start.20 = (f32[128,768]{1,0:T(8,128)S(1)}, f32[128,768]{1,0:T(8,128)}, u32[]{:S(2)}) copy-start(f32[128,768]{1,0:T(8,128)} %copy-done.19) | copy-start | bytes 1179652
  4377.2 71.2 %copy-start.70 = (f32[128]{0:T(128)S(1)}, f32[128]{0:T(128)}, u32[]{:S(2)}) copy-start(f32[128]{0:T(128)} %copy-done.69) | copy-start | bytes 1540
  (67 other events, 236.8 us)
Sparse Core Ops, SparseCore 0:
  9.6 52.0 all-gather.7
  78.7 36.9 all-gather.9
  117.3 21.0 all-gather.11
  139.8 62.6 all-gather.13
  203.8 62.6 all-gather.15
  3508.2 56.8 reduce-scatter.21
  4143.2 16.6 reduce-scatter.23
  4162.7 20.0 reduce-scatter.15
  4185.6 60.0 reduce-scatter.19
  4248.5 60.0 reduce-scatter.17
  4311.4 47.7 reduce-scatter.13
  4361.8 11.0 reduce-scatter.25
  4376.9 152.9 all-reduce.10
where the time goes:
time: 4560 us; the launch traced here: 4550 us
  local copies, waits for them, and re-layouts  2060 us (45%)
  other arithmetic  2010 us (44%)
  waiting for transfers between devices  279 us (6%)
  blocking collectives  124 us (3%)
  matrix products  45.6 us (1%)
    unnamed x15, other arithmetic  1800 us
    gather x1, local copies, waits for them, and re-layouts, tile_scores(): pair_pick = pairs_full[rows_at, head_ids]  940 us
    gather x3, local copies, waits for them, and re-layouts, tile_scores(): far_scores = far_scores + gates_full[rows_at, head_ids]  847 us
    unnamed x195, local copies, waits for them, and re-layouts  200 us
  transfers between devices with their start and end apart: 16, of which 8 were waited for; matrix products, arithmetic and copies ran while one was open for 57% of the time, Pallas kernels for 0%

commit v1 on v0

v1 whole, which is shorter than its diff:
```python
import functools

import jax
import jax.numpy as jnp
from jax import lax
from jax.experimental import pallas as pl
from jax.experimental.pallas import tpu as pltpu
from jax.sharding import PartitionSpec as P

H = 12
HD = 64
WIN = 64
LANES = 128
SLOT = 2048


EPSILON = 1e-05


def layer_norm(values, gain):
    mean_value = jnp.mean(values, axis=-1, keepdims=True)
    centred = values - mean_value
    variance = jnp.mean(centred * centred, axis=-1, keepdims=True)
    return centred * lax.rsqrt(variance + EPSILON) * gain


def tanh_gelu(values):
    return jax.nn.gelu(values, approximate=True)


def contract_rows(left, right):
    return lax.dot_general(
        left, right, (((0,), (0,)), ((), ())), preferred_element_type=jnp.float32
    )


def contract_cols(left, right):
    return lax.dot_general(
        left, right, (((1,), (1,)), ((), ())), preferred_element_type=jnp.float32
    )


NT = (((1,), (1,)), ((), ()))


def attend_body(tiles, base, idx_ref, q_ref, kv_ref, gate_ref, out_ref, prob_ref, score_ref, pair_ref):
    rows = q_ref.shape[0]
    span = tiles * LANES
    f32, bf16 = jnp.float32, jnp.bfloat16
    score_ref[:, :span] = (
        lax.dot_general(q_ref[...], kv_ref[:span, :], NT, preferred_element_type=f32) * HD ** (-0.5)
        + gate_ref[0, :, :span]
    )
    kept = idx_ref[0, 0]
    pair_ref[...] = jnp.concatenate([kept, kept], axis=1)
    wide = 8 * HD
    sub = lax.broadcasted_iota(jnp.int32, (8, wide), 0)
    lane = lax.broadcasted_iota(jnp.int32, (8, wide), 1)
    own = (lane // HD) == sub
    subf = sub.astype(f32)
    ahead = lax.broadcasted_iota(jnp.int32, (8, LANES), 0) - lax.broadcasted_iota(jnp.int32, (8, LANES), 1)
    near_from = max(0, tiles - 5)

    def eight(start):
        four = pair_ref[pl.ds(start, 8), :]
        index = jnp.concatenate([four] * 4, axis=1)
        pos = base + start + sub
        high = jnp.where(own & (pos >= WIN), index >> 7, -2).astype(f32)
        low = jnp.sum(jnp.where(own, (index & 127).astype(f32), 0.0), axis=0, keepdims=True) - subf
        high_pair = jnp.concatenate([high, high - 1.0], axis=0).astype(bf16)
        low_pair = jnp.concatenate([low, low - 8.0], axis=0).astype(bf16)
        one, zero = jnp.ones((), bf16), jnp.zeros((), bf16)
        left = jnp.concatenate(
            [jnp.where(high_pair == jnp.array(2 * p, bf16), one, zero) for p in range(tiles // 2)], axis=0
        )
        right = jnp.concatenate(
            [jnp.where(low_pair == jnp.array(16 * p, bf16), one, zero) for p in range(8)], axis=0
        )
        count = lax.dot_general(left, right, NT, preferred_element_type=f32)
        gap = ahead + (base + start)
        masked, counts = [], []
        largest = None
        for tile in range(tiles):
            number = count[8 * tile : 8 * tile + 8, :]
            if tile >= near_from:
                far = gap - tile * LANES
                number = number + jnp.where((far >= 0) & (far < WIN), 1.0, 0.0)
            value = jnp.where(number > 0.0, score_ref[pl.ds(start, 8), tile * LANES : (tile + 1) * LANES], -1e30)
            counts.append(number)
            masked.append(value)
            largest = value if largest is None else jnp.maximum(largest, value)
        top = jnp.max(largest, axis=1, keepdims=True)
        total = None
        expos = []
        for number, value in zip(counts, masked):
            expo = jnp.exp(value - top) * number
            expos.append(expo)
            total = expo if total is None else total + expo
        inverse = 1.0 / jnp.sum(total, axis=1, keepdims=True)
        return [expo * inverse for expo in expos]

    def step(index, carry):
        start = pl.multiple_of(index * 16, 16)
        first, second = eight(start), eight(start + 8)
        for tile in range(tiles):
            prob_ref[0, 0, pl.ds(start, 16), tile * LANES : (tile + 1) * LANES] = jnp.concatenate(
                [first[tile], second[tile]], axis=0
            ).astype(bf16)
        return carry

    lax.fori_loop(0, rows // 16, step, 0)
    both = jnp.dot(prob_ref[0, 0, :, :span], kv_ref[:span, :], preferred_element_type=f32)
    out_ref[0] = both[:, HD:].astype(bf16)


def attend_kernel(parts, chunk, base_ref, *refs):
    part = pl.program_id(1)
    base = base_ref[0] + part * chunk
    for at in range(parts):
        pl.when(part == at)(
            functools.partial(attend_body, (at + 1) * chunk // LANES, base, *refs)
        )


def attend(base, kept, query, pairs, gates):
    heads, parts, block, keep = kept.shape
    slot = pairs.shape[0]
    chunk = slot // parts
    grid_spec = pltpu.PrefetchScalarGridSpec(
        num_scalar_prefetch=1,
        grid=(heads, parts),
        in_specs=[
            pl.BlockSpec((1, 1, block, keep), lambda h, r, b: (h, r, 0, 0)),
            pl.BlockSpec((block, LANES), lambda h, r, b: (r, h)),
            pl.BlockSpec((slot, LANES), lambda h, r, b: (0, h)),
            pl.BlockSpec((1, 1, slot), lambda h, r, b: (h, 0, 0)),
        ],
        out_specs=[
            pl.BlockSpec((1, block, HD), lambda h, r, b: (h, r, 0)),
            pl.BlockSpec((1, 1, block, slot), lambda h, r, b: (h, r, 0, 0)),
        ],
        scratch_shapes=[pltpu.VMEM((block, slot), jnp.float32), pltpu.VMEM((block, 2 * keep), jnp.int32)],
    )
    return pl.pallas_call(
        functools.partial(attend_kernel, parts, chunk),
        grid_spec=grid_spec,
        out_shape=[
            jax.ShapeDtypeStruct((heads, parts * block, HD), jnp.bfloat16),
            jax.ShapeDtypeStruct((heads, parts, block, slot), jnp.bfloat16),
        ],
        name="attend",
    )(base, kept, query, pairs, gates)


def attend_back_body(first, tiles, chunk, q_ref, grad_ref, kv_ref, prob_ref, dq_ref, dkv_ref, gate_ref, raw_ref):
    f32, bf16 = jnp.float32, jnp.bfloat16
    rows = q_ref.shape[0]
    steps = tiles * LANES // chunk
    if first:
        dkv_ref[...] = jnp.zeros_like(dkv_ref)
        gate_ref[...] = jnp.zeros_like(gate_ref)
    dot_sum = None
    for at in range(steps):
        cols = slice(at * chunk, (at + 1) * chunk)
        raw = lax.dot_general(grad_ref[...], kv_ref[cols, :], NT, preferred_element_type=f32)
        raw_ref[:, cols] = raw
        part = jnp.sum(raw * prob_ref[0, 0, :, cols].astype(f32), axis=1, keepdims=True)
        dot_sum = part if dot_sum is None else dot_sum + part
    lane = lax.broadcasted_iota(jnp.int32, (rows, LANES), 1)
    scaled = jnp.where(lane == HD, 1.0, q_ref[...].astype(f32) * HD ** (-0.5))
    query_t = jnp.transpose(scaled)[: HD + 16].astype(bf16)
    grad_t = jnp.transpose(grad_ref[...].astype(f32))[HD:].astype(bf16)
    dq = None
    for at in range(steps):
        cols = slice(at * chunk, (at + 1) * chunk)
        prob = prob_ref[0, 0, :, cols]
        grad_score = (prob.astype(f32) * (raw_ref[:, cols] - dot_sum)).astype(bf16)
        piece = jnp.dot(grad_score, kv_ref[cols, :], preferred_element_type=f32)
        dq = piece if dq is None else dq + piece
        keys = jnp.dot(query_t, grad_score, preferred_element_type=f32)
        dkv_ref[0, :HD, cols] += keys[:HD]
        gate_ref[0, :, cols] += keys[HD : HD + 8]
        dkv_ref[0, HD:, cols] += jnp.dot(grad_t, prob, preferred_element_type=f32)
    dq_ref[0] = (dq[:, :HD] * HD ** (-0.5)).astype(dq_ref.dtype)


def attend_back_kernel(parts, chunk, *refs):
    part = pl.program_id(1)
    for at in range(parts):
        pl.when(part == at)(
            functools.partial(attend_back_body, at == 0, (at + 1) * chunk // LANES, chunk, *refs)
        )


def attend_back(query, grad, pairs, prob):
    heads, parts, block, slot = prob.shape
    chunk = slot // parts
    return pl.pallas_call(
        functools.partial(attend_back_kernel, parts, chunk),
        grid=(heads, parts),
        in_specs=[
            pl.BlockSpec((block, LANES), lambda h, r: (r, h)),
            pl.BlockSpec((block, LANES), lambda h, r: (r, h)),
            pl.BlockSpec((slot, LANES), lambda h, r: (0, h)),
            pl.BlockSpec((1, 1, block, slot), lambda h, r: (h, r, 0, 0)),
        ],
        out_specs=[
            pl.BlockSpec((1, block, HD), lambda h, r: (h, r, 0)),
            pl.BlockSpec((1, LANES, slot), lambda h, r: (h, 0, 0)),
            pl.BlockSpec((1, 8, slot), lambda h, r: (h, 0, 0)),
        ],
        out_shape=[
            jax.ShapeDtypeStruct((heads, parts * block, HD), jnp.float32),
            jax.ShapeDtypeStruct((heads, LANES, slot), jnp.float32),
            jax.ShapeDtypeStruct((heads, 8, slot), jnp.float32),
        ],
        scratch_shapes=[pltpu.VMEM((block, slot), jnp.float32)],
        name="attend_back",
    )(query, grad, pairs, prob)


def per_device(
    tokens,
    cotangent,
    lengths,
    kept_keys,
    first_gain,
    qkv_weight,
    score_weight,
    out_weight,
    second_gain,
    fc_weight,
    proj_weight,
):
    gathered = (
        lax.all_gather(first_gain, "dp", axis=0, tiled=True),
        lax.all_gather(qkv_weight, "dp", axis=0, tiled=True),
        lax.all_gather(score_weight, "dp", axis=0, tiled=True),
        lax.all_gather(out_weight, "dp", axis=0, tiled=True),
        lax.all_gather(second_gain, "dp", axis=0, tiled=True),
        lax.all_gather(fc_weight, "dp", axis=0, tiled=True),
        lax.all_gather(proj_weight, "dp", axis=0, tiled=True),
    )
    gain_one, qkv_full, score_full, out_full, gain_two, fc_full, proj_full = gathered
    gain_one = gain_one.astype(jnp.float32)
    gain_two = gain_two.astype(jnp.float32)
    seg_count = lax.axis_size("sp")
    ctx_count = lax.axis_size("ctx")
    local_rows = tokens.shape[1]
    heads_here = H // seg_count
    segment = SLOT // seg_count
    ctx_at = lax.axis_index("ctx")
    positions = (lax.axis_index("sp") * ctx_count + ctx_at) * local_rows + jnp.arange(
        local_rows, dtype=jnp.int32
    )
    is_valid = positions < lengths[0]
    inputs = tokens[0].astype(jnp.float32)
    norm_one = layer_norm(inputs, gain_one).astype(jnp.bfloat16)
    qkv_rows = jnp.dot(norm_one, qkv_full, preferred_element_type=jnp.float32).astype(jnp.bfloat16)
    key_score = jnp.dot(norm_one, score_full, preferred_element_type=jnp.float32).astype(
        jnp.bfloat16
    )
    head_qkv, head_score = (
        lax.all_to_all(qkv_rows, "sp", split_axis=1, concat_axis=0, tiled=True),
        lax.all_to_all(key_score, "sp", split_axis=1, concat_axis=0, tiled=True),
    )
    triple = head_qkv.reshape(seg_count, local_rows, heads_here, 3 * HD)
    queries = triple[..., :HD]
    pairs = triple[..., HD:].reshape(seg_count, local_rows, heads_here * 2 * HD)
    local_scores = head_score.reshape(seg_count, local_rows, heads_here)
    all_pairs, all_scores = (
        lax.all_gather(pairs, "ctx", axis=1, tiled=True),
        lax.all_gather(local_scores, "ctx", axis=1, tiled=True),
    )
    pairs_full = all_pairs.reshape(SLOT, heads_here * 2 * HD)
    raw_scores = all_scores.reshape(SLOT, heads_here).astype(jnp.float32)
    gates_full = -jnp.log1p(jnp.exp(-raw_scores)).T[:, None]
    kept = jnp.transpose(kept_keys[0], (2, 0, 1, 3))
    query_rows = seg_count * local_rows
    query_wide = jnp.pad(queries, ((0, 0), (0, 0), (0, 0), (0, HD))).reshape(
        query_rows, heads_here * LANES
    )
    base = (ctx_at * local_rows).astype(jnp.int32)[None]
    head_outs, prob = attend(base, kept, query_wide, pairs_full, gates_full)
    attended_heads = jnp.transpose(head_outs, (1, 0, 2))
    attended = lax.all_to_all(
        attended_heads.reshape(seg_count * local_rows, heads_here * HD),
        "sp",
        split_axis=0,
        concat_axis=1,
        tiled=True,
    )
    mixed = inputs + jnp.dot(attended, out_full, preferred_element_type=jnp.float32)
    norm_two = layer_norm(mixed, gain_two).astype(jnp.bfloat16)
    hidden_pre = jnp.dot(norm_two, fc_full, preferred_element_type=jnp.float32)
    active = tanh_gelu(hidden_pre).astype(jnp.bfloat16)
    result = jnp.where(
        is_valid[:, None],
        mixed + jnp.dot(active, proj_full, preferred_element_type=jnp.float32),
        0.0,
    )
    output = result.astype(jnp.bfloat16)[None]
    grad_out = jnp.where(is_valid[:, None], cotangent[0], jnp.zeros_like(cotangent[0]))
    proj_grad = contract_rows(active, grad_out)
    grad_active = contract_cols(grad_out, proj_full)
    _, gelu_pull = jax.vjp(tanh_gelu, hidden_pre)
    grad_pre = gelu_pull(grad_active)[0].astype(jnp.bfloat16)
    fc_grad = contract_rows(norm_two, grad_pre)
    grad_norm_two = contract_cols(grad_pre, fc_full)
    _, second_pull = jax.vjp(layer_norm, mixed, gain_two)
    grad_mixed_norm, second_gain_grad = second_pull(grad_norm_two)
    grad_mixed = grad_out.astype(jnp.float32) + grad_mixed_norm
    grad_branch = grad_mixed.astype(jnp.bfloat16)
    out_grad = contract_rows(attended, grad_branch)
    grad_attended = contract_cols(grad_branch, out_full).astype(jnp.bfloat16)
    head_grad = lax.all_to_all(grad_attended, "sp", split_axis=1, concat_axis=0, tiled=True)
    grad_wide = jnp.pad(
        head_grad.reshape(query_rows, heads_here, HD), ((0, 0), (0, 0), (HD, 0))
    ).reshape(query_rows, heads_here * LANES)
    query_grads, pair_grads, gate_grads = attend_back(query_wide, grad_wide, pairs_full, prob)
    grad_queries = jnp.transpose(query_grads, (1, 0, 2)).reshape(
        seg_count, local_rows, heads_here, HD
    )
    pair_grad = jnp.transpose(pair_grads, (2, 0, 1)).reshape(
        seg_count, segment, heads_here * 2 * HD
    )
    gate_total = gate_grads[:, 0].T.reshape(seg_count, segment, heads_here)
    pair_mine, gate_mine = (
        lax.psum_scatter(pair_grad, "ctx", scatter_dimension=1, tiled=True),
        lax.psum_scatter(gate_total, "ctx", scatter_dimension=1, tiled=True),
    )
    score_here = local_scores.astype(jnp.float32)
    grad_key_score = (gate_mine * jax.nn.sigmoid(-score_here)).astype(jnp.bfloat16)
    grad_triple = jnp.concatenate(
        [grad_queries, pair_mine.reshape(seg_count, local_rows, heads_here, 2 * HD)], axis=-1
    )
    grad_triple = grad_triple.astype(jnp.bfloat16).reshape(
        seg_count * local_rows, heads_here * 3 * HD
    )
    grad_qkv, grad_score = (
        lax.all_to_all(grad_triple, "sp", split_axis=0, concat_axis=1, tiled=True),
        lax.all_to_all(
            grad_key_score.reshape(seg_count * local_rows, heads_here),
            "sp",
            split_axis=0,
            concat_axis=1,
            tiled=True,
        ),
    )
    qkv_grad = contract_rows(norm_one, grad_qkv)
    score_grad = contract_rows(norm_one, grad_score)
    grad_norm_one = contract_cols(grad_qkv, qkv_full) + contract_cols(grad_score, score_full)
    _, first_pull = jax.vjp(layer_norm, inputs, gain_one)
    grad_input_norm, first_gain_grad = first_pull(grad_norm_one)
    input_grad = (grad_mixed + grad_input_norm).astype(jnp.bfloat16)[None]
    shards = (
        lax.psum_scatter(
            first_gain_grad.astype(jnp.bfloat16), "dp", scatter_dimension=0, tiled=True
        ).astype(jnp.float32),
        lax.psum_scatter(
            qkv_grad.astype(jnp.bfloat16), "dp", scatter_dimension=0, tiled=True
        ).astype(jnp.float32),
        lax.psum_scatter(
            score_grad.astype(jnp.bfloat16), "dp", scatter_dimension=0, tiled=True
        ).astype(jnp.float32),
        lax.psum_scatter(
            out_grad.astype(jnp.bfloat16), "dp", scatter_dimension=0, tiled=True
        ).astype(jnp.float32),
        lax.psum_scatter(
            second_gain_grad.astype(jnp.bfloat16), "dp", scatter_dimension=0, tiled=True
        ).astype(jnp.float32),
        lax.psum_scatter(
            fc_grad.astype(jnp.bfloat16), "dp", scatter_dimension=0, tiled=True
        ).astype(jnp.float32),
        lax.psum_scatter(
            proj_grad.astype(jnp.bfloat16), "dp", scatter_dimension=0, tiled=True
        ).astype(jnp.float32),
    )
    reduced = (
        lax.psum(shards[0].astype(jnp.bfloat16), ("sp", "ctx")).astype(jnp.float32),
        lax.psum(shards[1].astype(jnp.bfloat16), ("sp", "ctx")).astype(jnp.float32),
        lax.psum(shards[2].astype(jnp.bfloat16), ("sp", "ctx")).astype(jnp.float32),
        lax.psum(shards[3].astype(jnp.bfloat16), ("sp", "ctx")).astype(jnp.float32),
        lax.psum(shards[4].astype(jnp.bfloat16), ("sp", "ctx")).astype(jnp.float32),
        lax.psum(shards[5].astype(jnp.bfloat16), ("sp", "ctx")).astype(jnp.float32),
        lax.psum(shards[6].astype(jnp.bfloat16), ("sp", "ctx")).astype(jnp.float32),
    )
    return (
        output,
        input_grad,
        reduced[0],
        reduced[1],
        reduced[2],
        reduced[3],
        reduced[4],
        reduced[5],
        reduced[6],
    )


def solution(mesh):
    placed = (
        P("dp", ("sp", "ctx"), None),
        P("dp", ("sp", "ctx"), None),
        P("dp"),
        P("dp", None, "ctx", "sp", None),
        P("dp"),
        P("dp", None),
        P("dp", None),
        P("dp", None),
        P("dp"),
        P("dp", None),
        P("dp", None),
    )
    return jax.shard_map(
        per_device,
        mesh=mesh,
        in_specs=placed,
        out_specs=(
            P("dp", ("sp", "ctx"), None),
            P("dp", ("sp", "ctx"), None),
            P("dp"),
            P("dp", None),
            P("dp", None),
            P("dp", None),
            P("dp"),
            P("dp", None),
            P("dp", None),
        ),
        check_vma=False,
    )
```

time: 4560 us -> 909 us (0.20)
  other arithmetic: 2010 us -> 16.1 us
  local copies, waits for them, and re-layouts: 2060 us -> 203 us
  waiting for transfers between devices: 279 us -> 436 us
  Pallas kernels: 0 us -> 62.8 us
    unnamed x15 -> x0, other arithmetic: 1800 us -> none
    gather x17 -> x0, local copies, waits for them, and re-layouts: 1800 us -> none  [the longest x1 940 us: tile_scores(): pair_pick = pairs_full[rows_at, head_ids]]
    scatter-add x3 -> x0, other arithmetic: 163 us -> none  [the longest x1 78.2 us: backward_tile(): key_grad.at[rows_here]]
    pallas_call x0 -> x2, Pallas kernels: none -> 62.8 us  [the longest x1 48.9 us: attend(): pl.pallas_call(functools.partial(attend_kernel, parts, chunk), grid_spec=...]
    all_gather x1, waiting for transfers between devices: 0.02 us -> 60.9 us  [per_device(): lax.all_gather(proj_weight, 'dp', axis=0, tiled=True)]
    unnamed x195 -> x98, local copies, waits for them, and re-layouts: 200 us -> 190 us
  transfers between devices with their start and end apart: 16 -> 15, of which waited for: 8 -> 11; matrix products, arithmetic and copies ran while one was open for 57% -> 9% of each run, Pallas kernels for 0% -> 5%
where the time goes in v1:
time: 909 us; the launch traced here: 908 us
  waiting for transfers between devices  436 us (48%)
  local copies, waits for them, and re-layouts  203 us (22%)
  blocking collectives  132 us (15%)
  Pallas kernels  62.8 us (7%)
  matrix products  34.9 us (4%)
  other arithmetic  16.1 us (2%)
  between operations  15.9 us (2%)
    unnamed x98, local copies, waits for them, and re-layouts  190 us
    psum x1, waiting for transfers between devices, per_device(): lax.psum(shards[1].astype(jnp.bfloat16), ('sp', 'ctx')).astype(jnp.float32)  80.7 us
    psum x1, blocking collectives, per_device(): lax.psum(shards[0].astype(jnp.bfloat16), ('sp', 'ctx')).astype(jnp.float32)  63.5 us
    reduce_scatter x1, waiting for transfers between devices, per_device(): lax.psum_scatter(proj_grad.astype(jnp.bfloat16), 'dp', scatter_dimension=...  62.8 us
    all_gather x1, waiting for transfers between devices, per_device(): lax.all_gather(proj_weight, 'dp', axis=0, tiled=True)  60.9 us
    unnamed x16, waiting for transfers between devices  54.9 us
    reduce_scatter x1, waiting for transfers between devices, per_device(): lax.psum_scatter(qkv_grad.astype(jnp.bfloat16), 'dp', scatter_dimension=0...  50.6 us
    pallas_call x1, Pallas kernels, attend(): pl.pallas_call(functools.partial(attend_kernel, parts, chunk), grid_spec=...  48.9 us
  transfers between devices with their start and end apart: 15, of which 11 were waited for; matrix products, arithmetic and copies ran while one was open for 9% of the time, Pallas kernels for 5%

profile of v1, /device:TPU:0, one launch (start us, length us, event | category | flops | bytes accessed | tf_op | source)
XLA Modules:
  0.0 907.7 jit_solution(14361315928339617088)
XLA Ops:
  8.0 5.3 all-gather
  13.7 48.0 %all-gather.8.cloned.1.call-done = bf16[768,2304]{1,0:T(8,128)(2,1)} async-done(((bf16[384,2304]{1,0:T(8,128)(2,1)}), bf16[768,2304]{1,0:T(8,128)(2,1)}) %all-gather.8.cloned.1.call-update) | async-done | bytes 3538960 | tf_op jit(solution)/shard_map/all_gather | solution.py:237
  64.6 12.1 %all_to_all.99 = bf16[128,4,576]{0,2,1:T(8,128)(2,1)S(1)} all-to-all(bf16[128,4,576]{0,2,1:T(8,128)(2,1)S(1)} %bitcast.146), channel_id=1, replica_groups=mesh['dp'=2,'sp'=4,'ctx'=4] {'sp'}, dimensions={1} | all-to-all | bytes 1179648 | tf_op jit(solution)/shard_map/all_to_all | solution.py:264
  79.6 4.4 all_gather.30
  89.3 4.3 all-gather.1
  93.7 11.2 %all_gather.31 = bf16[4,512,3]{1,2,0:T(4,128)(2,1)S(1)} all-gather(bf16[4,128,3]{1,2,0:T(4,128)(2,1)S(1)} %bitcast.160), channel_id=1, replica_groups=mesh['dp'=2,'sp'=4,'ctx'=4] {'ctx'}, dimensions={1}, use_global_device_ids=true | all-gather | bytes 15360 | tf_op jit(solution)/shard_map/all_gather | solution.py:273
  106.7 8.1 all-gather.10.cloned.1.call-done
  117.3 48.9 %attend.1 = (bf16[3,512,64]{2,1,0:T(8,128)(2,1)}, bf16[3,4,128,2048]{3,2,1,0:T(8,128)(2,1)}) custom-call(s32[1]{0:T(128)} %bitcast.2.base_ref, s32[3,4,128,64]{3,2,1,0:T(8,128)} %bitcast.144, bf16[512,384]{1,0:T(8,128)(2,1)} %bitcast.140, bf16[2048,384]{1,0:T(8,128)(2,1)} %bitcast.135, f32[3,1,2048]{2,1,0:T(1,128)} %neg.22.refs_3_), custom_call_target="tpu_custom_call" | custom-call | tf_op jit(solution)/shard_map/attend/pallas_call | solution.py:144
  172.4 4.5 all-to-all-done.2
  178.9 22.7 %all-gather.14.cloned.1.call-done = bf16[768,3072]{1,0:T(8,128)(2,1)} async-done(((bf16[384,3072]{1,0:T(8,128)(2,1)}), bf16[768,3072]{1,0:T(8,128)(2,1)}) %all-gather.14.cloned.1.call-update) | async-done | bytes 4718608 | tf_op jit(solution)/shard_map/all_gather | solution.py:241
  204.7 60.9 %all-gather.16.cloned.1.call-done = bf16[3072,768]{1,0:T(8,128)(2,1)} async-done(((bf16[1536,768]{1,0:T(8,128)(2,1)}), bf16[3072,768]{1,0:T(8,128)(2,1)}) %all-gather.16.cloned.1.call-update) | async-done | bytes 4718608 | tf_op jit(solution)/shard_map/all_gather | solution.py:242
  265.6 4.4 fusion.6
  274.8 7.9 all_to_all.100
  283.9 13.9 %attend_back.1 = (f32[3,512,64]{2,1,0:T(8,128)}, f32[3,128,2048]{2,1,0:T(8,128)}, f32[3,8,2048]{2,1,0:T(8,128)}) custom-call(bf16[512,384]{1,0:T(8,128)(2,1)} %bitcast.141, bf16[512,384]{1,0:T(8,128)(2,1)} %copy.49.refs_1_, bf16[2048,384]{1,0:T(8,128)(2,1)} %bitcast.136, bf16[3,4,128,2048]{3,2,1,0:T(8,128)(2,1)} %get-tuple-element.15.refs_3_), custom_call_target="tpu_custom_call" | custom-call | tf_op jit(solution)/shard_map/attend_back/pallas_call | solution.py:198
  297.7 3.9 reshape.195
  301.6 48.2 %copy.53 = f32[4,512,384]{0,2,1:T(8,128)} copy(f32[4,512,384]{1,0,2:T(4,128)S(1)} %reshape.195) | data formatting | bytes 6291456
  349.9 89.4 %reshape.205 = f32[512,1536]{1,0:T(8,128)} reshape(f32[512,384,4]{2,1,0:T(8,128)} %bitcast.37) | data formatting | bytes 6291456
  443.7 3.7 convolution_convert_fusion.1
  448.8 3.8 convolution_convert_fusion
  454.3 44.6 %reduce-scatter.22.cloned.1.call-done = f32[128,1536]{1,0:T(8,128)} async-done(((f32[512,1536]{1,0:T(8,128)}), f32[128,1536]{1,0:T(8,128)}) %reduce-scatter.22.cloned.1.call-update) | async-done | bytes 786448
  498.9 29.1 %reshape.206 = bf16[128,384,4]{2,1,0:T(8,128)(2,1)} reshape(f32[128,1536]{1,0:T(8,128)} %reduce-scatter.22.cloned.1.call-done) | data formatting | bytes 1179648
  528.0 12.1 %copy.54 = bf16[4,128,384]{1,0,2:T(4,128)(2,1)S(1)} copy(bf16[4,128,384]{0,2,1:T(8,128)(2,1)} %bitcast.134) | data formatting | bytes 786432
  540.2 12.2 %all_to_all.101 = bf16[4,128,576]{1,2,0:T(8,128)(2,1)S(1)} all-to-all(bf16[4,128,576]{1,2,0:T(8,128)(2,1)S(1)} %bitcast.145), channel_id=1, replica_groups=mesh['dp'=2,'sp'=4,'ctx'=4] {'sp'}, dimensions={0} | all-to-all | bytes 1179648 | tf_op jit(solution)/shard_map/all_to_all | solution.py:341
  556.7 6.1 all_to_all.102
  564.0 42.9 %reduce-scatter.18.cloned.1.call-done = bf16[384,3072]{1,0:T(8,128)(2,1)} async-done(((bf16[768,3072]{1,0:T(8,128)(2,1)}), bf16[384,3072]{1,0:T(8,128)(2,1)}) %reduce-scatter.18.cloned.1.call-update) | async-done | bytes 2359312 | tf_op jit(solution)/shard_map/reduce_scatter | solution.py:372
  607.0 62.8 %reduce-scatter.20.cloned.1.call-done = bf16[1536,768]{1,0:T(8,128)(2,1)} async-done(((bf16[3072,768]{1,0:T(8,128)(2,1)}), bf16[1536,768]{1,0:T(8,128)(2,1)}) %reduce-scatter.20.cloned.1.call-update) | async-done | bytes 2359312 | tf_op jit(solution)/shard_map/reduce_scatter | solution.py:375
  669.8 50.6 %reduce-scatter.14.cloned.1.call-done = bf16[384,2304]{1,0:T(8,128)(2,1)} async-done(((bf16[768,2304]{1,0:T(8,128)(2,1)}), bf16[384,2304]{1,0:T(8,128)(2,1)}) %reduce-scatter.14.cloned.1.call-update) | async-done | bytes 1769488 | tf_op jit(solution)/shard_map/reduce_scatter | solution.py:360
  722.3 4.1 fusion.9
  726.3 7.8 reduce-scatter.26.cloned.1.call-done
  739.1 4.9 all-reduce.5
  744.2 63.5 %all-reduce.3 = (bf16[384]{0:T(512)(128)(2,1)S(1)}, bf16[384,12]{0,1:T(8,128)(2,1)S(1)}, bf16[384]{0:T(512)(128)(2,1)S(1)}) all-reduce(bf16[384]{0:T(512)(128)(2,1)S(1)} %dynamic-slice.1, bf16[384,12]{0,1:T(8,128)(2,1)S(1)} %copy.58, bf16[384]{0:T(512)(128)(2,1)S(1)} %dynamic-slice.3), channel_id=1, replica_groups=mesh['dp'=2,'sp'=4,'ctx'=4] {'sp','ctx'}, use_global_device_ids=true, to_apply=%region_12.13 | all-reduce | flops 5376 | bytes 21504 | tf_op jit(solution)/shard_map/psum | solution.py:380
  810.4 80.7 %all-reduce.8.cloned.1.call-done = (bf16[384,2304]{1,0:T(8,128)(2,1)}, bf16[384,768]{1,0:T(8,128)(2,1)}, bf16[384,3072]{1,0:T(8,128)(2,1)}, bf16[1536,768]{1,0:T(8,128)(2,1)}) async-done(((bf16[384,2304]{1,0:T(8,128)(2,1)}, bf16[384,768]{1,0:T(8,128)(2,1)}, bf16[384,3072]{1,0:T(8,128)(2,1)}, bf16[1536,768]{1,0:T(8,128)(2,1)}), (bf16[384,2304]{1,0:T(8,128)(2,1)}, bf16[384,768]{1,0:T(8,128)(2,1)}, ...) | async-done | bytes 7077904 | tf_op jit(solution)/shard_map/psum | solution.py:381
  (186 shorter events, 65.0 us)
Async XLA Ops:
  7.2 6.1 copy-start.1
  7.2 54.4 %all-gather.8.cloned.1.call-start = ((), (), s32[]{:S(2)}) async-start(), calls=%async_computation.13 | async-start | bytes 5308416 | tf_op jit(solution)/shard_map/all_gather | solution.py:237
  7.9 106.8 %all-gather.10.cloned.1.call-start = ((), (), s32[]{:S(2)}) async-start(), calls=%async_computation.14 | async-start | bytes 1966080 | tf_op jit(solution)/shard_map/all_gather | solution.py:272
  13.7 48.0 %copy-start.36 = (f32[128]{0:T(128)}, f32[128]{0:T(128)S(1)}, u32[]{:S(2)}) copy-start(f32[128]{0:T(128)S(1)} %fusion.19) | copy-start | bytes 1540
  13.7 70.3 %copy-start.27 = (f32[128]{0:T(128)}, f32[128]{0:T(128)S(1)}, u32[]{:S(2)}) copy-start(f32[128]{0:T(128)S(1)} %fusion.28) | copy-start | bytes 1540
  64.3 12.4 %copy-start.38 = (pred[128]{0:T(512)(128)(4,1)S(1)}, pred[128]{0:T(512)(128)(4,1)}, u32[]{:S(2)}) copy-start(pred[128]{0:T(512)(128)(4,1)} %constant.34.clone.1) | copy-start | bytes 388
  77.6 94.8 %all-gather.12.cloned.1.call-start = ((), (), s32[]{:S(2)}) async-start(), calls=%async_computation.15 | async-start | bytes 1769472 | tf_op jit(solution)/shard_map/all_gather | solution.py:239
  78.3 123.2 %all-gather.14.cloned.1.call-start = ((), (), s32[]{:S(2)}) async-start(), calls=%async_computation.16 | async-start | bytes 7077888 | tf_op jit(solution)/shard_map/all_gather | solution.py:241
  78.9 9.2 %copy-start.19 = (s32[1,4,128,3,64]{2,4,3,1,0:T(8,128)S(1)}, s32[1,4,128,3,64]{2,4,3,1,0:T(8,128)}, u32[]{:S(2)}) copy-start(s32[1,4,128,3,64]{2,4,3,1,0:T(8,128)} %param.14) | copy-start | bytes 1179652
  78.9 10.4 %copy-start.35 = (bf16[384]{0:T(512)(128)(2,1)S(1)}, bf16[384]{0:T(512)(128)(2,1)}, u32[]{:S(2)}) copy-start(bf16[384]{0:T(512)(128)(2,1)} %param.19) | copy-start | bytes 2308
  78.9 186.7 %all-gather.16.cloned.1.call-start = ((), (), s32[]{:S(2)}) async-start(), calls=%async_computation.17 | async-start | bytes 7077888 | tf_op jit(solution)/shard_map/all_gather | solution.py:242
  84.0 21.6 %copy-start.20 = (bf16[768,12]{0,1:T(8,128)(2,1)}, bf16[768,12]{0,1:T(8,128)(2,1)S(1)}, u32[]{:S(2)}) copy-start(bf16[768,12]{0,1:T(8,128)(2,1)S(1)} %all_gather.30) | copy-start | bytes 55300
  84.9 8.8 all-to-all-start.1
  168.2 8.6 all-to-all-start.2
  171.6 327.3 %reduce-scatter.22.cloned.1.call-start = ((), (), s32[]{:S(2)}) async-start(), calls=%async_computation.22 | async-start | bytes 3932160
  172.3 100.2 %copy-start.30 = (pred[128]{0:T(512)(128)(4,1)}, pred[128]{0:T(512)(128)(4,1)S(1)}, u32[]{:S(2)}) copy-start(pred[128]{0:T(512)(128)(4,1)S(1)} %add_compare_fusion) | copy-start | bytes 388
  178.6 93.7 %copy-start.22 = (f32[128]{0:T(128)}, f32[128]{0:T(128)S(1)}, u32[]{:S(2)}) copy-start(f32[128]{0:T(128)S(1)} %broadcast_multiply_fusion) | copy-start | bytes 1540
  178.8 93.5 %copy-start.24 = (f32[128]{0:T(128)}, f32[128]{0:T(128)S(1)}, u32[]{:S(2)}) copy-start(f32[128]{0:T(128)S(1)} %fusion.29) | copy-start | bytes 1540
  178.9 86.7 %copy-start.16 = (bf16[1,128,768]{2,1,0:T(8,128)(2,1)S(1)}, bf16[1,128,768]{2,1,0:T(8,128)(2,1)}, u32[]{:S(2)}) copy-start(bf16[1,128,768]{2,1,0:T(8,128)(2,1)} %param.12) | copy-start | bytes 589828
  204.7 65.3 %copy-start.3 = (f32[128,3072]{1,0:T(8,128)}, f32[128,3072]{1,0:T(8,128)S(1)}, u32[]{:S(2)}) copy-start(f32[128,3072]{1,0:T(8,128)S(1)} %fusion.36) | copy-start | bytes 4718596
  272.5 10.1 %copy-start.32 = (f32[128]{0:T(128)}, f32[128]{0:T(128)S(1)}, u32[]{:S(2)}) copy-start(f32[128]{0:T(128)S(1)} %negate_multiply_fusion.1) | copy-start | bytes 1540
  439.3 116.3 %reduce-scatter.24.cloned.1.call-start = ((), (), s32[]{:S(2)}) async-start(), calls=%async_computation.23 | async-start | bytes 327680
  442.0 122.0 %reduce-scatter.16.cloned.1.call-start = ((), (), s32[]{:S(2)}) async-start(), calls=%async_computation.19 | async-start | bytes 1769472 | tf_op jit(solution)/shard_map/reduce_scatter | solution.py:366
  443.6 163.4 %reduce-scatter.18.cloned.1.call-start = ((), (), s32[]{:S(2)}) async-start(), calls=%async_computation.20 | async-start | bytes 7077888 | tf_op jit(solution)/shard_map/reduce_scatter | solution.py:372
  447.4 222.4 %reduce-scatter.20.cloned.1.call-start = ((), (), s32[]{:S(2)}) async-start(), calls=%async_computation.21 | async-start | bytes 7077888 | tf_op jit(solution)/shard_map/reduce_scatter | solution.py:375
  452.6 267.8 %reduce-scatter.14.cloned.1.call-start = ((), (), s32[]{:S(2)}) async-start(), calls=%async_computation.18 | async-start | bytes 5308416 | tf_op jit(solution)/shard_map/reduce_scatter | solution.py:360
  540.1 12.4 %copy-start.2 = (bf16[1,128,768]{2,1,0:T(8,128)(2,1)S(1)}, bf16[1,128,768]{2,1,0:T(8,128)(2,1)}, u32[]{:S(2)}) copy-start(bf16[1,128,768]{2,1,0:T(8,128)(2,1)} %param.11) | copy-start | bytes 589828
  540.1 12.4 %copy-start.28 = (f32[128]{0:T(128)S(1)}, f32[128]{0:T(128)}, u32[]{:S(2)}) copy-start(f32[128]{0:T(128)} %copy-done.27) | copy-start | bytes 1540
  555.5 178.6 %reduce-scatter.26.cloned.1.call-start = ((), (), s32[]{:S(2)}) async-start(), calls=%async_computation.24 | async-start | bytes 294912
  564.0 327.2 %all-reduce.8.cloned.1.call-start = ((), (), s32[]{:S(2)}) async-start(), calls=%async_computation.25 | async-start | bytes 14155776 | tf_op jit(solution)/shard_map/psum | solution.py:381
  738.4 71.1 %copy-start.7 = (f32[128,768]{1,0:T(8,128)S(1)}, f32[128,768]{1,0:T(8,128)}, u32[]{:S(2)}) copy-start(f32[128,768]{1,0:T(8,128)} %copy-done.6) | copy-start | bytes 1179652
  738.4 71.1 %copy-start.33 = (f32[128]{0:T(128)S(1)}, f32[128]{0:T(128)}, u32[]{:S(2)}) copy-start(f32[128]{0:T(128)} %copy-done.32) | copy-start | bytes 1540
  (23 other events, 47.8 us)
Sparse Core Ops, SparseCore 0:
  9.6 52.0 all-gather.7
  77.7 37.0 all-gather.9
  116.3 20.9 all-gather.11
  138.7 62.7 all-gather.13
  202.9 62.6 all-gather.15
  439.4 59.4 reduce-scatter.21
  501.1 19.8 reduce-scatter.23
  523.9 20.0 reduce-scatter.15
  546.8 60.0 reduce-scatter.17
  609.7 60.0 reduce-scatter.19
  672.6 47.7 reduce-scatter.13
  723.0 11.0 reduce-scatter.25
  738.1 152.9 all-reduce.7

commit v2 on v1

v2 whole, which is shorter than its diff:
```python
import functools

import jax
import jax.numpy as jnp
from jax import lax
from jax.experimental import pallas as pl
from jax.experimental.pallas import tpu as pltpu
from jax.sharding import PartitionSpec as P

H = 12
HD = 64
WIN = 64
LANES = 128
SLOT = 2048


EPSILON = 1e-05


def layer_norm(values, gain):
    mean_value = jnp.mean(values, axis=-1, keepdims=True)
    centred = values - mean_value
    variance = jnp.mean(centred * centred, axis=-1, keepdims=True)
    return centred * lax.rsqrt(variance + EPSILON) * gain


def tanh_gelu(values):
    return jax.nn.gelu(values, approximate=True)


def contract_rows(left, right):
    return lax.dot_general(
        left, right, (((0,), (0,)), ((), ())), preferred_element_type=jnp.float32
    )


def contract_cols(left, right):
    return lax.dot_general(
        left, right, (((1,), (1,)), ((), ())), preferred_element_type=jnp.float32
    )


NT = (((1,), (1,)), ((), ()))


PAD_ROWS = 16


def slot_order(src_ref, kv_ref):
    count, height, _ = src_ref.shape
    for tile in range(kv_ref.shape[0] // LANES):
        part, at = divmod(tile, count)
        kv_ref[tile * LANES : (tile + 1) * LANES, :] = src_ref[at, part * LANES : (part + 1) * LANES, :]


def slot_gates(src_ref, gate_ref):
    count, height, _ = src_ref.shape
    for at in range(count):
        scores = src_ref[at, height - PAD_ROWS :, :].astype(jnp.float32)
        gates = -jnp.log1p(jnp.exp(-scores))
        for part in range(gate_ref.shape[1] // LANES // count):
            tile = part * count + at
            gate_ref[:, tile * LANES : (tile + 1) * LANES] = jnp.broadcast_to(gates[part : part + 1, :], (8, LANES))


def attend_body(first, tiles, base, idx_ref, q_ref, src_ref, out_ref, prob_ref, score_ref, pair_ref, kv_ref, gate_ref):
    rows = q_ref.shape[0]
    if first:
        slot_order(src_ref, kv_ref)
        slot_gates(src_ref, gate_ref)
    span = tiles * LANES
    f32, bf16 = jnp.float32, jnp.bfloat16
    score_ref[:, :span] = (
        lax.dot_general(q_ref[...], kv_ref[:span, :], NT, preferred_element_type=f32) * HD ** (-0.5)
        + gate_ref[0:1, :span]
    )
    kept = idx_ref[0, 0]
    pair_ref[...] = jnp.concatenate([kept, kept], axis=1)
    wide = 8 * HD
    sub = lax.broadcasted_iota(jnp.int32, (8, wide), 0)
    lane = lax.broadcasted_iota(jnp.int32, (8, wide), 1)
    own = (lane // HD) == sub
    subf = sub.astype(f32)
    ahead = lax.broadcasted_iota(jnp.int32, (8, LANES), 0) - lax.broadcasted_iota(jnp.int32, (8, LANES), 1)
    near_from = max(0, tiles - 5)

    def eight(start):
        four = pair_ref[pl.ds(start, 8), :]
        index = jnp.concatenate([four] * 4, axis=1)
        pos = base + start + sub
        high = jnp.where(own & (pos >= WIN), index >> 7, -2).astype(f32)
        low = jnp.sum(jnp.where(own, (index & 127).astype(f32), 0.0), axis=0, keepdims=True) - subf
        high_pair = jnp.concatenate([high, high - 1.0], axis=0).astype(bf16)
        low_pair = jnp.concatenate([low, low - 8.0], axis=0).astype(bf16)
        one, zero = jnp.ones((), bf16), jnp.zeros((), bf16)
        left = jnp.concatenate(
            [jnp.where(high_pair == jnp.array(2 * p, bf16), one, zero) for p in range(tiles // 2)], axis=0
        )
        right = jnp.concatenate(
            [jnp.where(low_pair == jnp.array(16 * p, bf16), one, zero) for p in range(8)], axis=0
        )
        count = lax.dot_general(left, right, NT, preferred_element_type=f32)
        gap = ahead + (base + start)
        masked, counts = [], []
        largest = None
        for tile in range(tiles):
            number = count[8 * tile : 8 * tile + 8, :]
            if tile >= near_from:
                far = gap - tile * LANES
                number = number + jnp.where((far >= 0) & (far < WIN), 1.0, 0.0)
            value = jnp.where(number > 0.0, score_ref[pl.ds(start, 8), tile * LANES : (tile + 1) * LANES], -1e30)
            counts.append(number)
            masked.append(value)
            largest = value if largest is None else jnp.maximum(largest, value)
        top = jnp.max(largest, axis=1, keepdims=True)
        total = None
        expos = []
        for number, value in zip(counts, masked):
            expo = jnp.exp(value - top) * number
            expos.append(expo)
            total = expo if total is None else total + expo
        inverse = 1.0 / jnp.sum(total, axis=1, keepdims=True)
        return [expo * inverse for expo in expos]

    def step(index, carry):
        start = pl.multiple_of(index * 16, 16)
        first, second = eight(start), eight(start + 8)
        for tile in range(tiles):
            prob_ref[0, 0, pl.ds(start, 16), tile * LANES : (tile + 1) * LANES] = jnp.concatenate(
                [first[tile], second[tile]], axis=0
            ).astype(bf16)
        return carry

    lax.fori_loop(0, rows // 16, step, 0)
    both = jnp.dot(prob_ref[0, 0, :, :span], kv_ref[:span, :], preferred_element_type=f32)
    out_ref[0] = both[:, HD:].astype(bf16)


def attend_kernel(parts, chunk, base_ref, *refs):
    part = pl.program_id(1)
    base = base_ref[0] + part * chunk
    for at in range(parts):
        pl.when(part == at)(
            functools.partial(attend_body, at == 0, (at + 1) * chunk // LANES, base, *refs)
        )


def attend(base, kept, query, pairs):
    heads, parts, block, keep = kept.shape
    count, height, _ = pairs.shape
    slot = count * (height - PAD_ROWS)
    chunk = slot // parts
    grid_spec = pltpu.PrefetchScalarGridSpec(
        num_scalar_prefetch=1,
        grid=(heads, parts),
        in_specs=[
            pl.BlockSpec((1, 1, block, keep), lambda h, r, b: (h, r, 0, 0)),
            pl.BlockSpec((block, LANES), lambda h, r, b: (r, h)),
            pl.BlockSpec((count, height, LANES), lambda h, r, b: (0, 0, h)),
        ],
        out_specs=[
            pl.BlockSpec((1, block, HD), lambda h, r, b: (h, r, 0)),
            pl.BlockSpec((1, 1, block, slot), lambda h, r, b: (h, r, 0, 0)),
        ],
        scratch_shapes=[
            pltpu.VMEM((block, slot), jnp.float32),
            pltpu.VMEM((block, 2 * keep), jnp.int32),
            pltpu.VMEM((slot, LANES), jnp.bfloat16),
            pltpu.VMEM((8, slot), jnp.float32),
        ],
    )
    return pl.pallas_call(
        functools.partial(attend_kernel, parts, chunk),
        grid_spec=grid_spec,
        out_shape=[
            jax.ShapeDtypeStruct((heads, parts * block, HD), jnp.bfloat16),
            jax.ShapeDtypeStruct((heads, parts, block, slot), jnp.bfloat16),
        ],
        name="attend",
    )(base, kept, query, pairs)


def attend_back_body(first, last, tiles, chunk, q_ref, grad_ref, src_ref, prob_ref, dq_ref, out_ref, raw_ref, kv_ref, dkv_ref, gate_ref):
    f32, bf16 = jnp.float32, jnp.bfloat16
    rows = q_ref.shape[0]
    steps = tiles * LANES // chunk
    if first:
        slot_order(src_ref, kv_ref)
        dkv_ref[...] = jnp.zeros_like(dkv_ref)
        gate_ref[...] = jnp.zeros_like(gate_ref)
    dot_sum = None
    for at in range(steps):
        cols = slice(at * chunk, (at + 1) * chunk)
        raw = lax.dot_general(grad_ref[...], kv_ref[cols, :], NT, preferred_element_type=f32)
        raw_ref[:, cols] = raw
        part = jnp.sum(raw * prob_ref[0, 0, :, cols].astype(f32), axis=1, keepdims=True)
        dot_sum = part if dot_sum is None else dot_sum + part
    lane = lax.broadcasted_iota(jnp.int32, (rows, LANES), 1)
    scaled = jnp.where(lane == HD, 1.0, q_ref[...].astype(f32) * HD ** (-0.5))
    query_t = jnp.transpose(scaled)[: HD + 16].astype(bf16)
    grad_t = jnp.transpose(grad_ref[...].astype(f32))[HD:].astype(bf16)
    dq = None
    for at in range(steps):
        cols = slice(at * chunk, (at + 1) * chunk)
        prob = prob_ref[0, 0, :, cols]
        grad_score = (prob.astype(f32) * (raw_ref[:, cols] - dot_sum)).astype(bf16)
        piece = jnp.dot(grad_score, kv_ref[cols, :], preferred_element_type=f32)
        dq = piece if dq is None else dq + piece
        keys = jnp.dot(query_t, grad_score, preferred_element_type=f32)
        dkv_ref[:HD, cols] += keys[:HD]
        gate_ref[:, cols] += keys[HD : HD + 8]
        dkv_ref[HD:, cols] += jnp.dot(grad_t, prob, preferred_element_type=f32)
    dq_ref[...] = (dq * HD ** (-0.5)).astype(dq_ref.dtype)
    if last:
        count, height, _ = out_ref.shape
        parts = (height - PAD_ROWS) // LANES
        for at in range(count):
            rows_of = []
            for part in range(parts):
                cols = slice((part * count + at) * LANES, (part * count + at + 1) * LANES)
                out_ref[at, part * LANES : (part + 1) * LANES, :] = jnp.transpose(dkv_ref[:, cols]).astype(bf16)
                rows_of.append(gate_ref[0:1, cols])
            rows_of.append(jnp.zeros((PAD_ROWS - parts, LANES), f32))
            out_ref[at, height - PAD_ROWS :, :] = jnp.concatenate(rows_of, axis=0).astype(bf16)


def attend_back_kernel(parts, chunk, *refs):
    part = pl.program_id(1)
    for at in range(parts):
        pl.when(part == at)(
            functools.partial(attend_back_body, at == 0, at == parts - 1, (at + 1) * chunk // LANES, chunk, *refs)
        )


def attend_back(query, grad, pairs, prob):
    heads, parts, block, slot = prob.shape
    count, height, width = pairs.shape
    chunk = slot // parts
    return pl.pallas_call(
        functools.partial(attend_back_kernel, parts, chunk),
        grid=(heads, parts),
        in_specs=[
            pl.BlockSpec((block, LANES), lambda h, r: (r, h)),
            pl.BlockSpec((block, LANES), lambda h, r: (r, h)),
            pl.BlockSpec((count, height, LANES), lambda h, r: (0, 0, h)),
            pl.BlockSpec((1, 1, block, slot), lambda h, r: (h, r, 0, 0)),
        ],
        out_specs=[
            pl.BlockSpec((block, LANES), lambda h, r: (r, h)),
            pl.BlockSpec((count, height, LANES), lambda h, r: (0, 0, h)),
        ],
        out_shape=[
            jax.ShapeDtypeStruct((parts * block, heads * LANES), jnp.bfloat16),
            jax.ShapeDtypeStruct((count, height, width), jnp.bfloat16),
        ],
        scratch_shapes=[
            pltpu.VMEM((block, slot), jnp.float32),
            pltpu.VMEM((slot, LANES), jnp.bfloat16),
            pltpu.VMEM((LANES, slot), jnp.float32),
            pltpu.VMEM((8, slot), jnp.float32),
        ],
        name="attend_back",
    )(query, grad, pairs, prob)


def dp_gather(mine):
    if lax.axis_size("dp") != 2:
        return lax.all_gather(mine, "dp", axis=0, tiled=True)
    other = lax.ppermute(mine, "dp", [(0, 1), (1, 0)])
    return jnp.where(
        lax.axis_index("dp") == 0, jnp.concatenate([mine, other]), jnp.concatenate([other, mine])
    )


def dp_scatter(parts):
    if lax.axis_size("dp") != 2:
        return lax.psum_scatter(parts, "dp", scatter_dimension=0, tiled=False)
    at = lax.axis_index("dp")
    mine = lax.dynamic_index_in_dim(parts, at, 0, keepdims=False)
    sent = lax.dynamic_index_in_dim(parts, 1 - at, 0, keepdims=False)
    other = lax.ppermute(sent, "dp", [(0, 1), (1, 0)])
    return (mine.astype(jnp.float32) + other.astype(jnp.float32)).astype(parts.dtype)


def per_device(
    tokens,
    cotangent,
    lengths,
    kept_keys,
    first_gain,
    qkv_weight,
    score_weight,
    out_weight,
    second_gain,
    fc_weight,
    proj_weight,
):
    f32, bf16 = jnp.float32, jnp.bfloat16
    dp_count = lax.axis_size("dp")
    seg_count = lax.axis_size("sp")
    ctx_count = lax.axis_size("ctx")
    dp_at = lax.axis_index("dp")
    sp_at = lax.axis_index("sp")
    ctx_at = lax.axis_index("ctx")
    rows = tokens.shape[1]
    width = tokens.shape[2]
    group_rows = seg_count * rows
    heads = H // seg_count
    head_cols = heads * 3 * HD
    hidden = fc_weight.shape[1]
    hidden_part = hidden // (dp_count * seg_count)
    piece = width // (dp_count * ctx_count)

    own_in = jnp.concatenate(
        [
            lax.dynamic_slice_in_dim(qkv_weight, sp_at * head_cols, head_cols, 1),
            lax.dynamic_slice_in_dim(score_weight, sp_at * heads, heads, 1),
            first_gain[:, None],
            second_gain[:, None],
        ],
        axis=1,
    )
    all_in = dp_gather(own_in)
    tokens_group = lax.all_gather(tokens[0], "sp", axis=0, tiled=True)
    in_weight = all_in[:, : head_cols + heads]
    gain_one = all_in[:, head_cols + heads].astype(f32)
    gain_two = all_in[:, head_cols + heads + 1].astype(f32)

    out_own = out_weight
    fc_own = lax.dynamic_index_in_dim(
        fc_weight.reshape(width // dp_count, dp_count, seg_count, hidden_part), sp_at, 2, keepdims=False
    ).reshape(width // dp_count, dp_count * hidden_part)
    proj_own = lax.dynamic_slice_in_dim(proj_weight, sp_at * hidden_part, hidden_part, 0)
    all_in, out_own, fc_own, proj_own = lax.optimization_barrier((all_in, out_own, fc_own, proj_own))

    inputs = tokens[0].astype(f32)
    inputs_group = tokens_group.astype(f32)
    norm_one = layer_norm(inputs_group, gain_one).astype(bf16)
    qkv_rows = jnp.dot(norm_one, in_weight[:, :head_cols], preferred_element_type=f32).astype(bf16)
    key_score = lax.dot_general(
        in_weight[:, head_cols:], norm_one, (((0,), (1,)), ((), ())), preferred_element_type=f32
    ).astype(bf16)
    triple = qkv_rows.reshape(group_rows, heads, 3 * HD)
    score_rows = jnp.transpose(key_score.reshape(heads, seg_count, rows), (1, 0, 2)).reshape(
        seg_count, heads * rows
    )
    pairs_own = jnp.concatenate(
        [
            triple[..., HD:].reshape(group_rows, heads * 2 * HD),
            jnp.pad(score_rows, ((0, PAD_ROWS - seg_count), (0, 0))),
        ],
        axis=0,
    )
    pairs = lax.all_gather(pairs_own, "ctx", axis=0, tiled=False)
    query_wide = jnp.pad(triple[..., :HD], ((0, 0), (0, 0), (0, HD))).reshape(group_rows, heads * LANES)
    kept = jnp.transpose(kept_keys[0], (2, 0, 1, 3))
    base = (ctx_at * rows).astype(jnp.int32)[None]
    head_outs, prob = attend(base, kept, query_wide, pairs)
    attended = jnp.transpose(head_outs, (1, 0, 2)).reshape(group_rows, heads * HD)

    out_all = dp_gather(out_own)
    out_part = lax.dynamic_slice_in_dim(out_all, sp_at * heads * HD, heads * HD, 0)
    fc_part = dp_gather(fc_own)
    proj_part = dp_gather(proj_own)
    cot_group = lax.all_gather(cotangent[0], "sp", axis=0, tiled=True)
    group_at = jnp.arange(group_rows, dtype=jnp.int32)
    group_positions = (group_at // rows) * (ctx_count * rows) + ctx_at * rows + group_at % rows
    grad_out_group = jnp.where((group_positions < lengths[0])[:, None], cot_group, jnp.zeros_like(cot_group))
    positions = (sp_at * ctx_count + ctx_at) * rows + jnp.arange(rows, dtype=jnp.int32)
    is_valid = (positions < lengths[0])[:, None]

    branch = jnp.dot(attended, out_part, preferred_element_type=f32).astype(bf16)
    mixed = inputs + lax.psum_scatter(branch, "sp", scatter_dimension=0, tiled=True).astype(f32)
    norm_two_own = layer_norm(mixed, gain_two).astype(bf16)
    norm_two = lax.all_gather(norm_two_own, "sp", axis=0, tiled=True)
    hidden_pre = jnp.dot(norm_two, fc_part, preferred_element_type=f32)
    active = tanh_gelu(hidden_pre).astype(bf16)
    grad_active = contract_cols(grad_out_group, proj_part)
    _, gelu_pull = jax.vjp(tanh_gelu, hidden_pre)
    grad_pre = gelu_pull(grad_active)[0].astype(bf16)
    grad_norm_two = lax.psum_scatter(
        contract_cols(grad_pre, fc_part).astype(bf16), "sp", scatter_dimension=0, tiled=True
    ).astype(f32)
    _, second_pull = jax.vjp(layer_norm, mixed, gain_two)
    grad_mixed_norm, second_gain_grad = second_pull(grad_norm_two)
    grad_out = jnp.where(is_valid, cotangent[0], jnp.zeros_like(cotangent[0])).astype(f32)
    grad_mixed = grad_out + grad_mixed_norm
    grad_branch = lax.all_gather(grad_mixed.astype(bf16), "sp", axis=0, tiled=True)

    out_wide = jnp.pad(out_part.reshape(heads, HD, width), ((0, 0), (HD, 0), (0, 0))).reshape(heads * LANES, width)
    grad_wide = contract_cols(grad_branch, out_wide).astype(bf16)
    query_grads, pair_grads = attend_back(query_wide, grad_wide, pairs, prob)
    pair_mine = lax.psum_scatter(pair_grads, "ctx", scatter_dimension=0, tiled=False)

    expanded = lax.psum_scatter(
        jnp.dot(active, proj_part, preferred_element_type=f32).astype(bf16), "sp", scatter_dimension=0, tiled=True
    ).astype(f32)
    output = jnp.where(is_valid, mixed + expanded, 0.0).astype(bf16)[None]

    big = jnp.concatenate(
        [
            contract_rows(norm_two, grad_pre).astype(bf16).reshape(dp_count, ctx_count, piece, width),
            contract_rows(active, grad_out_group).astype(bf16).reshape(dp_count, ctx_count, -1, width),
            contract_rows(attended, grad_branch).astype(bf16).reshape(dp_count, ctx_count, -1, width),
        ],
        axis=2,
    )
    big_own = lax.psum_scatter(dp_scatter(big), "ctx", scatter_dimension=0, tiled=False)
    proj_piece = hidden // (seg_count * dp_count * ctx_count)
    both = piece + proj_piece
    out_piece = heads * HD // (dp_count * ctx_count)
    out_rows = dp_gather(big_own[both:])
    big_all = lax.all_gather(jnp.concatenate([big_own[:both], out_rows], axis=0), ("sp", "ctx"), axis=0, tiled=False)
    big_all = big_all.reshape(seg_count, ctx_count, both + dp_count * out_piece, width)
    fc_grad = jnp.transpose(
        big_all[:, :, :piece].reshape(seg_count, ctx_count, piece, dp_count, hidden_part), (1, 2, 3, 0, 4)
    ).reshape(width // dp_count, hidden).astype(f32)
    proj_grad = big_all[:, :, piece:both].reshape(hidden // dp_count, width).astype(f32)
    out_grad = jnp.transpose(
        big_all[:, :, both:].reshape(seg_count, ctx_count, dp_count, out_piece, width), (0, 2, 1, 3, 4)
    ).reshape(width, width)
    out_grad = lax.dynamic_slice_in_dim(out_grad, dp_at * (width // dp_count), width // dp_count, 0).astype(f32)

    grad_triple = jnp.concatenate(
        [
            query_grads.reshape(group_rows, heads, LANES)[..., :HD],
            pair_mine[:group_rows].reshape(group_rows, heads, 2 * HD),
        ],
        axis=-1,
    ).reshape(group_rows, head_cols)
    gate_rows = jnp.transpose(
        pair_mine[group_rows : group_rows + seg_count].reshape(seg_count, heads, rows), (1, 0, 2)
    ).reshape(heads, group_rows)
    grad_score = (gate_rows.astype(f32) * jax.nn.sigmoid(-key_score.astype(f32))).astype(bf16)
    grad_norm_part = contract_cols(grad_triple, in_weight[:, :head_cols]) + lax.dot_general(
        grad_score, in_weight[:, head_cols:], (((0,), (1,)), ((), ())), preferred_element_type=f32
    )
    grad_norm_one = lax.psum_scatter(grad_norm_part.astype(bf16), "sp", scatter_dimension=0, tiled=True).astype(f32)
    _, first_pull = jax.vjp(layer_norm, inputs, gain_one)
    grad_input_norm, first_gain_grad = first_pull(grad_norm_one)
    input_grad = (grad_mixed + grad_input_norm).astype(bf16)[None]

    small = jnp.concatenate(
        [
            contract_rows(norm_one, grad_triple).astype(bf16),
            lax.dot_general(norm_one, grad_score, (((0,), (1,)), ((), ())), preferred_element_type=f32).astype(bf16),
            first_gain_grad.astype(bf16)[:, None],
            second_gain_grad.astype(bf16)[:, None],
        ],
        axis=1,
    ).reshape(dp_count, ctx_count, piece, head_cols + heads + 2)
    small_own = lax.psum_scatter(dp_scatter(small), "ctx", scatter_dimension=0, tiled=False)
    small_all = lax.all_gather(small_own, ("sp", "ctx"), axis=0, tiled=False).reshape(
        seg_count, ctx_count * piece, head_cols + heads + 2
    )
    qkv_grad = jnp.transpose(small_all[:, :, :head_cols], (1, 0, 2)).reshape(-1, seg_count * head_cols).astype(f32)
    score_grad = jnp.transpose(small_all[:, :, head_cols : head_cols + heads], (1, 0, 2)).reshape(-1, H).astype(f32)
    gains = jnp.sum(small_all[:, :, head_cols + heads :].astype(f32), axis=0)
    return (output, input_grad, gains[:, 0], qkv_grad, score_grad, out_grad, gains[:, 1], fc_grad, proj_grad)


def solution(mesh):
    placed = (
        P("dp", ("sp", "ctx"), None),
        P("dp", ("sp", "ctx"), None),
        P("dp"),
        P("dp", None, "ctx", "sp", None),
        P("dp"),
        P("dp", None),
        P("dp", None),
        P("dp", None),
        P("dp"),
        P("dp", None),
        P("dp", None),
    )
    return jax.shard_map(
        per_device,
        mesh=mesh,
        in_specs=placed,
        out_specs=(
            P("dp", ("sp", "ctx"), None),
            P("dp", ("sp", "ctx"), None),
            P("dp"),
            P("dp", None),
            P("dp", None),
            P("dp", None),
            P("dp"),
            P("dp", None),
            P("dp", None),
        ),
        check_vma=False,
    )
```

time: 909 us -> 546 us (0.60)
  waiting for transfers between devices: 436 us -> 278 us
  local copies, waits for them, and re-layouts: 203 us -> 67.6 us
  blocking collectives: 132 us -> 33.4 us
  other arithmetic: 16.1 us -> 42.6 us
    unnamed x98 -> x73, local copies, waits for them, and re-layouts: 190 us -> 10.8 us
    psum x1 -> x0, waiting for transfers between devices: 80.7 us -> none  [per_device(): lax.psum(shards[1].astype(jnp.bfloat16), ('sp', 'ctx')).astype(jnp.float32)]
    psum x1 -> x0, blocking collectives: 63.5 us -> none  [per_device(): lax.psum(shards[0].astype(jnp.bfloat16), ('sp', 'ctx')).astype(jnp.float32)]
    unnamed x16 -> x10, waiting for transfers between devices: 54.9 us -> 0.16 us
    all_gather x5 -> x3, waiting for transfers between devices: 140 us -> 88.8 us  [the longest x1 42.5 us: per_device(): lax.all_gather(jnp.concatenate([big_own[:both], out_rows], axis=0), ('sp'...]
    ppermute x0 -> x7, waiting for transfers between devices: none -> 42 us  [the longest x2 25.8 us: dp_scatter(): other = lax.ppermute(sent, 'dp', [(0, 1), (1, 0)])]
    all_to_all x4 -> x0, blocking collectives: 38.3 us -> none  [the longest x1 12.2 us: per_device(): lax.all_to_all(grad_triple, 'sp', split_axis=0, concat_axis=1, tiled=True)]
    convert_element_type x4 -> x9, local copies, waits for them, and re-layouts: 0.48 us -> 28.2 us  [the longest x3 20.6 us: per_device(): fc_grad = jnp.transpose(big_all[:, :, :piece].reshape(seg_count, ctx_coun...]
  transfers between devices with their start and end apart: 15 -> 17, of which waited for: 11 -> 15; matrix products, arithmetic and copies ran while one was open for 9% -> 13% of each run, Pallas kernels for 5% -> 0%
where the time goes in v2:
time: 546 us; the launch traced here: 541 us
  waiting for transfers between devices  278 us (51%)
  local copies, waits for them, and re-layouts  67.6 us (12%)
  Pallas kernels  62.5 us (11%)
  other arithmetic  42.6 us (8%)
  blocking collectives  33.4 us (6%)
  matrix products  28.3 us (5%)
  between operations  15.7 us (3%)
  starting transfers between devices  12.6 us (2%)
    pallas_call x1, Pallas kernels, attend(): pl.pallas_call(functools.partial(attend_kernel, parts, chunk), grid_spec=...  48.8 us
    all_gather x1, waiting for transfers between devices, per_device(): lax.all_gather(jnp.concatenate([big_own[:both], out_rows], axis=0), ('sp'...  42.5 us
    all_gather x1, waiting for transfers between devices, per_device(): lax.all_gather(small_own, ('sp', 'ctx'), axis=0, tiled=False)  35.6 us
    reduce_scatter x1, waiting for transfers between devices, per_device(): lax.psum_scatter(pair_grads, 'ctx', scatter_dimension=0, tiled=False)  35.2 us
    reduce_scatter x1, waiting for transfers between devices, per_device(): lax.psum_scatter(dp_scatter(big), 'ctx', scatter_dimension=0, tiled=False)  32.7 us
    ppermute x2, waiting for transfers between devices, dp_scatter(): other = lax.ppermute(sent, 'dp', [(0, 1), (1, 0)])  25.8 us
    reduce_scatter x1, waiting for transfers between devices, per_device(): lax.psum_scatter(jnp.dot(active, proj_part, preferred_element_type=f32).a...  24.4 us
    convert_element_type x3, local copies, waits for them, and re-layouts, per_device(): fc_grad = jnp.transpose(big_all[:, :, :piece].reshape(seg_count, ctx_coun...  20.6 us
  transfers between devices with their start and end apart: 17, of which 15 were waited for; matrix products, arithmetic and copies ran while one was open for 13% of the time, Pallas kernels for 0%

profile of v2, /device:TPU:0, one launch (start us, length us, event | category | flops | bytes accessed | tf_op | source)
XLA Modules:
  0.0 540.6 jit_solution(12556036075327988136)
XLA Ops:
  15.2 8.6 %all-gather = bf16[1,512,768]{2,1,0:T(8,128)(2,1)S(1)} all-gather(bf16[1,128,768]{2,1,0:T(8,128)(2,1)S(1)} %copy-done.2), channel_id=2, replica_groups=mesh['dp'=2,'sp'=4,'ctx'=4] {'sp'}, dimensions={1}, use_global_device_ids=true | all-gather | bytes 983040 | tf_op jit(solution)/shard_map/all_gather | solution.py:324
  34.5 5.5 %reshape.254 = bf16[384,2,4,384]{3,2,1,0:T(4,128)(2,1)} reshape(bf16[384,3072]{1,0:T(8,128)(2,1)} %param.20) | data formatting | bytes 4718592 | tf_op jit(solution)/shard_map/reshape | solution.py:331
  40.0 5.8 %dynamic-slice_reduce_fusion = bf16[384,2,384]{2,1,0:T(2,128)(2,1)S(1)} fusion(bf16[384,2,4,384]{3,2,1,0:T(4,128)(2,1)} %reshape.254, s32[]{:T(128)S(6)} %select_n.98), kind=kLoop, calls=%fused_computation.42 | loop fusion | bytes 1179652 | tf_op jit(solution)/shard_map/jit(dynamic_index_in_dim)/dynamic_slice | solution.py:330
  51.4 10.9 %collective-permute-done.1 = bf16[384,768]{1,0:T(8,128)(2,1)S(1)} collective-permute-done((bf16[384,768]{1,0:T(8,128)(2,1)}, bf16[384,768]{1,0:T(8,128)(2,1)S(1)}, u32[]{:S(2)}, u32[]{:S(2)}) %collective-permute-start.1) | collective-permute-done | bytes 589856 | tf_op jit(solution)/shard_map/ppermute | solution.py:269
  62.7 10.7 %all-gather.10.cloned.1.call-done = bf16[2112,384]{1,0:T(8,128)(2,1)} async-done(((bf16[528,384]{1,0:T(8,128)(2,1)}), bf16[2112,384]{1,0:T(8,128)(2,1)}) %all-gather.10.cloned.1.call-update) | async-done | bytes 1622032 | tf_op jit(solution)/shard_map/all_gather | solution.py:354
  73.4 48.8 %attend.1 = (bf16[3,512,64]{2,1,0:T(8,128)(2,1)}, bf16[3,4,128,2048]{3,2,1,0:T(8,128)(2,1)}) custom-call(s32[1]{0:T(128)} %bitcast.2.base_ref, s32[3,4,128,64]{3,2,1,0:T(8,128)} %bitcast.180, bf16[512,384]{1,0:T(8,128)(2,1)} %copy.75.refs_1_.refs_0_, bf16[4,528,384]{2,1,0:T(8,128)(2,1)} %bitcast.171), custom_call_target="tpu_custom_call" | custom-call | tf_op jit(solution)/shard_map/attend/pallas_call | solution.py:172
  125.5 8.6 %all-gather.2 = bf16[1,512,768]{2,1,0:T(8,128)(2,1)S(1)} all-gather(bf16[1,128,768]{2,1,0:T(8,128)(2,1)S(1)} %copy-done.12), channel_id=4, replica_groups=mesh['dp'=2,'sp'=4,'ctx'=4] {'sp'}, dimensions={1}, use_global_device_ids=true | all-gather | bytes 983040 | tf_op jit(solution)/shard_map/all_gather | solution.py:365
  136.1 10.9 %reduce-scatter.8.cloned.1.call-done = bf16[128,768]{1,0:T(8,128)(2,1)} async-done(((bf16[512,768]{1,0:T(8,128)(2,1)}), bf16[128,768]{1,0:T(8,128)(2,1)}) %reduce-scatter.8.cloned.1.call-update) | async-done | bytes 196624 | tf_op jit(solution)/shard_map/reduce_scatter | solution.py:373
  150.2 8.2 %all_gather.30 = bf16[512,768]{1,0:T(8,128)(2,1)S(1)} all-gather(bf16[128,768]{1,0:T(8,128)(2,1)S(1)} %multiply_convert_fusion.1), channel_id=1, replica_groups=mesh['dp'=2,'sp'=4,'ctx'=4] {'sp'}, dimensions={0}, use_global_device_ids=true | all-gather | bytes 983040 | tf_op jit(solution)/shard_map/all_gather | solution.py:375
  169.4 3.8 convolution_convert_fusion.4
  173.4 19.1 %reduce-scatter.12.cloned.1.call-done = bf16[128,768]{1,0:T(8,128)(2,1)} async-done(((bf16[512,768]{1,0:T(8,128)(2,1)}), bf16[128,768]{1,0:T(8,128)(2,1)}) %reduce-scatter.12.cloned.1.call-update) | async-done | bytes 196624 | tf_op jit(solution)/shard_map/reduce_scatter | solution.py:381
  194.3 24.4 %reduce-scatter.10.cloned.1.call-done = bf16[128,768]{1,0:T(8,128)(2,1)} async-done(((bf16[512,768]{1,0:T(8,128)(2,1)}), bf16[128,768]{1,0:T(8,128)(2,1)}) %reduce-scatter.10.cloned.1.call-update) | async-done | bytes 196624 | tf_op jit(solution)/shard_map/reduce_scatter | solution.py:395
  220.8 8.0 %all_gather.32 = bf16[512,768]{1,0:T(8,128)(2,1)S(1)} all-gather(bf16[128,768]{1,0:T(8,128)(2,1)S(1)} %fusion.40), channel_id=1, replica_groups=mesh['dp'=2,'sp'=4,'ctx'=4] {'sp'}, dimensions={0}, use_global_device_ids=true | all-gather | bytes 983040 | tf_op jit(solution)/shard_map/all_gather | solution.py:388
  230.2 13.7 %attend_back.1 = (bf16[512,384]{1,0:T(8,128)(2,1)}, bf16[4,528,384]{2,1,0:T(8,128)(2,1)}) custom-call(bf16[512,384]{1,0:T(8,128)(2,1)} %copy.75.refs_1_.refs_0_, bf16[512,384]{1,0:T(8,128)(2,1)} %convolution_convert_fusion.7.refs_1_, bf16[4,528,384]{2,1,0:T(8,128)(2,1)} %bitcast.172, bf16[3,4,128,2048]{3,2,1,0:T(8,128)(2,1)} %get-tuple-element.20.refs_3_), custom_call_target="tpu_custom_call" | custom-call | tf_op jit(solution)/shard_map/attend_back/pallas_call | solution.py:239
  245.8 35.2 %reduce-scatter.14.cloned.1.call-done = bf16[1,528,384]{2,1,0:T(8,128)(2,1)} async-done(((bf16[4,528,384]{2,1,0:T(8,128)(2,1)}), bf16[1,528,384]{2,1,0:T(8,128)(2,1)}) %reduce-scatter.14.cloned.1.call-update) | async-done | bytes 405520 | tf_op jit(solution)/shard_map/reduce_scatter | solution.py:393
  285.3 3.1 add_convert_fusion
  288.8 3.3 convolution_convert_fusion.1
  303.8 7.0 %reduce-scatter.16.cloned.1.call-done = bf16[128,768]{1,0:T(8,128)(2,1)} async-done(((bf16[512,768]{1,0:T(8,128)(2,1)}), bf16[128,768]{1,0:T(8,128)(2,1)}) %reduce-scatter.16.cloned.1.call-update) | async-done | bytes 196624 | tf_op jit(solution)/shard_map/reduce_scatter | solution.py:438
  315.4 25.8 %collective-permute-done.4 = bf16[4,96,581]{2,1,0:T(8,128)(2,1)S(1)} collective-permute-done((bf16[4,96,581]{2,1,0:T(8,128)(2,1)S(1)}, bf16[4,96,581]{2,1,0:T(8,128)(2,1)S(1)}, u32[]{:S(2)}, u32[]{:S(2)}) %collective-permute-start.4) | collective-permute-done | bytes 446240 | tf_op jit(solution)/shard_map/ppermute | solution.py:281
  342.2 3.1 fusion
  345.4 17.7 %reduce-scatter.18.cloned.1.call-done = bf16[1,96,581]{2,1,0:T(8,128)(2,1)} async-done(((bf16[4,96,581]{2,1,0:T(8,128)(2,1)}), bf16[1,96,581]{2,1,0:T(8,128)(2,1)}) %reduce-scatter.18.cloned.1.call-update) | async-done | bytes 111568 | tf_op jit(solution)/shard_map/reduce_scatter | solution.py:452
  363.4 32.7 %reduce-scatter.20.cloned.1.call-done = bf16[1,216,768]{2,1,0:T(8,128)(2,1)} async-done(((bf16[4,216,768]{2,1,0:T(8,128)(2,1)}), bf16[1,216,768]{2,1,0:T(8,128)(2,1)}) %reduce-scatter.20.cloned.1.call-update) | async-done | bytes 331792 | tf_op jit(solution)/shard_map/reduce_scatter | solution.py:408
  402.6 35.6 %all-gather.8.cloned.1.call-done = bf16[16,96,581]{2,1,0:T(8,128)(2,1)} async-done(((bf16[1,96,581]{2,1,0:T(8,128)(2,1)}), bf16[16,96,581]{2,1,0:T(8,128)(2,1)}) %all-gather.8.cloned.1.call-update) | async-done | bytes 1784848 | tf_op jit(solution)/shard_map/all_gather | solution.py:453
  438.1 3.7 convert_bitcast_fusion
  441.8 5.3 copy.85
  447.2 5.2 copy.89
  456.4 42.5 %all-gather.12.cloned.1.call-done = bf16[3840,768]{1,0:T(8,128)(2,1)} async-done(((bf16[240,768]{1,0:T(8,128)(2,1)}), bf16[3840,768]{1,0:T(8,128)(2,1)}) %all-gather.12.cloned.1.call-update) | async-done | bytes 5898256 | tf_op jit(solution)/shard_map/all_gather | solution.py:413
  500.3 6.0 %fusion.70 = (bf16[4,4,96,768]{3,2,1,0:T(8,128)(2,1)}, f32[4,4,96,768]{3,2,1,0:T(8,128)}) fusion(bf16[4,4,240,768]{3,2,1,0:T(8,128)(2,1)} %bitcast.174), kind=kLoop, calls=%fused_computation.154 | loop fusion | flops 1179648 | bytes 11796480 | tf_op jit(solution)/shard_map/slice | solution.py:418
  507.4 6.7 %reshape.278 = f32[4,4,96,2,384]{4,3,2,1,0:T(2,128)} reshape(f32[4,4,96,768]{3,2,1,0:T(8,128)} %get-tuple-element.63) | data formatting | bytes 9437184 | tf_op jit(solution)/shard_map/convert_element_type | solution.py:417
  514.1 7.6 %copy.100 = f32[4,4,96,2,384]{4,0,3,2,1:T(4,128)} copy(f32[4,4,96,2,384]{4,3,2,1,0:T(2,128)} %reshape.278) | data formatting | bytes 9437184 | tf_op jit(solution)/shard_map/convert_element_type | solution.py:417
  521.6 6.4 %reshape.275 = f32[384,3072]{1,0:T(8,128)} reshape(f32[4,96,2,4,384]{4,3,2,1,0:T(4,128)} %bitcast.169) | data formatting | bytes 9437184 | tf_op jit(solution)/shard_map/convert_element_type | solution.py:417
  528.0 4.4 bitcast_convert_fusion
  (186 shorter events, 86.8 us)
Async XLA Ops:
  7.2 39.6 %copy-start = (bf16[1536,768]{1,0:T(8,128)(2,1)S(1)}, bf16[1536,768]{1,0:T(8,128)(2,1)}, u32[]{:S(2)}) copy-start(bf16[1536,768]{1,0:T(8,128)(2,1)} %param.21) | copy-start | bytes 7077892
  7.2 8.0 %copy-start.2 = (bf16[1,128,768]{2,1,0:T(8,128)(2,1)S(1)}, bf16[1,128,768]{2,1,0:T(8,128)(2,1)}, u32[]{:S(2)}) copy-start(bf16[1,128,768]{2,1,0:T(8,128)(2,1)} %param.11) | copy-start | bytes 589828
  7.2 66.2 %all-gather.10.cloned.1.call-start = ((), (), s32[]{:S(2)}) async-start(), calls=%async_computation.15 | async-start | bytes 2027520 | tf_op jit(solution)/shard_map/all_gather | solution.py:354
  12.2 14.5 %collective-permute-start = (bf16[384,581]{1,0:T(8,128)(2,1)}, bf16[384,581]{1,0:T(8,128)(2,1)}, u32[]{:S(2)}, u32[]{:S(2)}) collective-permute-start(bf16[384,581]{1,0:T(8,128)(2,1)} %pad_maximum_fusion.3), channel_id=1, source_target_pairs={{0,16},{16,0},{1,17},{17,1},{2,18},{18,2},{3,19},{19,3},{4,20},{20... | collective-permute-start | bytes 1338632 | tf_op jit(solution)/shard_map/ppermute | solution.py:269
  34.0 113.0 %reduce-scatter.8.cloned.1.call-start = ((), (), s32[]{:S(2)}) async-start(), calls=%async_computation.7 | async-start | bytes 983040 | tf_op jit(solution)/shard_map/reduce_scatter | solution.py:373
  47.6 14.7 %copy-start.19 = (bf16[384,768]{1,0:T(8,128)(2,1)S(1)}, bf16[384,768]{1,0:T(8,128)(2,1)}, u32[]{:S(2)}) copy-start(bf16[384,768]{1,0:T(8,128)(2,1)} %param.18) | copy-start | bytes 1769476
  47.6 14.7 %collective-permute-start.1 = (bf16[384,768]{1,0:T(8,128)(2,1)}, bf16[384,768]{1,0:T(8,128)(2,1)S(1)}, u32[]{:S(2)}, u32[]{:S(2)}) collective-permute-start(bf16[384,768]{1,0:T(8,128)(2,1)} %param.18), channel_id=1, source_target_pairs={{0,16},{16,0},{1,17},{17,1},{2,18},{18,2},{3,19},{19,3},{4,20},{20... | collective-permute-start | bytes 1769480 | tf_op jit(solution)/shard_map/ppermute | solution.py:269
  123.4 12.1 %copy-start.20 = (bf16[384,768]{1,0:T(8,128)(2,1)S(1)}, bf16[384,768]{1,0:T(8,128)(2,1)}, u32[]{:S(2)}) copy-start(bf16[384,768]{1,0:T(8,128)(2,1)} %constant_dynamic-slice_fusion) | copy-start | bytes 1769476
  124.7 67.8 %reduce-scatter.12.cloned.1.call-start = ((), (), s32[]{:S(2)}) async-start(), calls=%async_computation.9 | async-start | bytes 983040 | tf_op jit(solution)/shard_map/reduce_scatter | solution.py:381
  125.4 37.1 %copy-start.30 = (pred[512]{0:T(512)(128)(4,1)}, pred[512]{0:T(512)(128)(4,1)S(1)}, u32[]{:S(2)}) copy-start(pred[512]{0:T(512)(128)(4,1)S(1)} %fusion.55) | copy-start | bytes 1540
  134.0 28.5 %copy-start.16 = (bf16[1,512,768]{2,1,0:T(8,128)(2,1)}, bf16[1,512,768]{2,1,0:T(8,128)(2,1)S(1)}, u32[]{:S(2)}) copy-start(bf16[1,512,768]{2,1,0:T(8,128)(2,1)S(1)} %all-gather.2) | copy-start | bytes 2359300
  134.0 24.4 %collective-permute-start.2 = (bf16[384,768]{1,0:T(8,128)(2,1)}, bf16[384,768]{1,0:T(8,128)(2,1)}, u32[]{:S(2)}, u32[]{:S(2)}) collective-permute-start(bf16[384,768]{1,0:T(8,128)(2,1)} %bitcast.197), channel_id=1, source_target_pairs={{0,16},{16,0},{1,17},{17,1},{2,18},{18,2},{3,19},{19,3},{4,20},{20... | collective-permute-start | bytes 1769480 | tf_op jit(solution)/shard_map/ppermute | solution.py:269
  135.5 27.1 %collective-permute-start.3 = (bf16[384,768]{1,0:T(8,128)(2,1)S(1)}, bf16[384,768]{1,0:T(8,128)(2,1)}, u32[]{:S(2)}, u32[]{:S(2)}) collective-permute-start(bf16[384,768]{1,0:T(8,128)(2,1)S(1)} %copy-done.20), channel_id=1, source_target_pairs={{0,16},{16,0},{1,17},{17,1},{2,18},{18,2},{3,19},{19,3},{4,20},{20... | collective-permute-start | bytes 1769480 | tf_op jit(solution)/shard_map/ppermute | solution.py:269
  169.4 49.3 %reduce-scatter.10.cloned.1.call-start = ((), (), s32[]{:S(2)}) async-start(), calls=%async_computation.8 | async-start | bytes 983040 | tf_op jit(solution)/shard_map/reduce_scatter | solution.py:395
  173.2 19.3 %copy-start.8 = (bf16[128,768]{1,0:T(8,128)(2,1)S(1)}, bf16[128,768]{1,0:T(8,128)(2,1)}, u32[]{:S(2)}) copy-start(bf16[128,768]{1,0:T(8,128)(2,1)} %reduce-scatter.8.cloned.1.call-done) | copy-start | bytes 589828
  173.3 107.7 %reduce-scatter.14.cloned.1.call-start = ((), (), s32[]{:S(2)}) async-start(), calls=%async_computation.10 | async-start | bytes 2027520 | tf_op jit(solution)/shard_map/reduce_scatter | solution.py:393
  173.3 47.4 %copy-start.24 = (pred[128]{0:T(512)(128)(4,1)}, pred[128]{0:T(512)(128)(4,1)S(1)}, u32[]{:S(2)}) copy-start(pred[128]{0:T(512)(128)(4,1)S(1)} %add_compare_fusion) | copy-start | bytes 388
  220.6 9.5 %copy-start.27 = (f32[128]{0:T(128)}, f32[128]{0:T(128)S(1)}, u32[]{:S(2)}) copy-start(f32[128]{0:T(128)S(1)} %negate_multiply_fusion.1) | copy-start | bytes 1540
  243.9 37.8 %copy-start.5 = (bf16[768,581]{1,0:T(8,128)(2,1)S(1)}, bf16[768,581]{1,0:T(8,128)(2,1)}, u32[]{:S(2)}) copy-start(bf16[768,581]{1,0:T(8,128)(2,1)} %copy-done.4) | copy-start | bytes 2677252
  243.9 66.9 %reduce-scatter.16.cloned.1.call-start = ((), (), s32[]{:S(2)}) async-start(), calls=%async_computation.11 | async-start | bytes 983040 | tf_op jit(solution)/shard_map/reduce_scatter | solution.py:438
  288.5 74.6 %reduce-scatter.18.cloned.1.call-start = ((), (), s32[]{:S(2)}) async-start(), calls=%async_computation.12 | async-start | bytes 614400 | tf_op jit(solution)/shard_map/reduce_scatter | solution.py:452
  299.9 42.2 %collective-permute-start.5 = (bf16[4,216,768]{2,1,0:T(8,128)(2,1)}, bf16[4,216,768]{2,1,0:T(8,128)(2,1)}, u32[]{:S(2)}, u32[]{:S(2)}) collective-permute-start(bf16[4,216,768]{2,1,0:T(8,128)(2,1)} %dynamic-slice_bitcast_fusion), channel_id=1, source_target_pairs={{0,16},{16,0},{1,17},{17,1},{2,18},{18,2},{3,19},{19,3},{4,20},{20... | collective-permute-start | bytes 3981320 | tf_op jit(solution)/shard_map/ppermute | solution.py:281
  302.5 8.3 %copy-start.26 = (f32[128]{0:T(128)S(1)}, f32[128]{0:T(128)}, u32[]{:S(2)}) copy-start(f32[128]{0:T(128)} %broadcast_multiply_fusion.1) | copy-start | bytes 1540
  303.1 10.4 %copy-start.15 = (bf16[768,3]{1,0:T(8,128)(2,1)S(1)}, bf16[768,3]{1,0:T(8,128)(2,1)}, u32[]{:S(2)}) copy-start(bf16[768,3]{1,0:T(8,128)(2,1)} %copy.90) | copy-start | bytes 13828
  313.8 27.4 %collective-permute-start.4 = (bf16[4,96,581]{2,1,0:T(8,128)(2,1)S(1)}, bf16[4,96,581]{2,1,0:T(8,128)(2,1)S(1)}, u32[]{:S(2)}, u32[]{:S(2)}) collective-permute-start(bf16[4,96,581]{2,1,0:T(8,128)(2,1)S(1)} %dynamic-slice_bitcast_fusion.1), channel_id=1, source_target_pairs={{0,16},{16,0},{1,17},{17,1},{2,18},{18,2},{3,19},{19,3},{4,20},{20... | collective-permute-start | bytes 1338632 | tf_op jit(solution)/shard_map/ppermute | solution.py:281
  342.1 53.9 %reduce-scatter.20.cloned.1.call-start = ((), (), s32[]{:S(2)}) async-start(), calls=%async_computation.14 | async-start | bytes 1658880 | tf_op jit(solution)/shard_map/reduce_scatter | solution.py:408
  345.3 56.3 %copy-start.11 = (bf16[128,768]{1,0:T(8,128)(2,1)S(1)}, bf16[128,768]{1,0:T(8,128)(2,1)}, u32[]{:S(2)}) copy-start(bf16[128,768]{1,0:T(8,128)(2,1)} %reduce-scatter.16.cloned.1.call-done) | copy-start | bytes 589828
  345.3 56.3 %copy-start.25 = (pred[128]{0:T(512)(128)(4,1)S(1)}, pred[128]{0:T(512)(128)(4,1)}, u32[]{:S(2)}) copy-start(pred[128]{0:T(512)(128)(4,1)} %copy-done.24) | copy-start | bytes 388
  345.3 56.3 %copy-start.28 = (f32[128]{0:T(128)S(1)}, f32[128]{0:T(128)}, u32[]{:S(2)}) copy-start(f32[128]{0:T(128)} %copy-done.27) | copy-start | bytes 1540
  345.3 92.8 %all-gather.8.cloned.1.call-start = ((), (), s32[]{:S(2)}) async-start(), calls=%async_computation.13 | async-start | bytes 2088960 | tf_op jit(solution)/shard_map/all_gather | solution.py:453
  363.1 135.9 %all-gather.12.cloned.1.call-start = ((), (), s32[]{:S(2)}) async-start(), calls=%async_computation.16 | async-start | bytes 6266880 | tf_op jit(solution)/shard_map/all_gather | solution.py:413
  396.8 4.0 collective-permute-start.6
  (21 other events, 59.5 us)
Sparse Core Ops, SparseCore 0:
  34.1 39.2 all-gather.9
  124.8 22.0 reduce-scatter.7
  169.5 22.9 reduce-scatter.11
  195.5 23.1 reduce-scatter.9
  244.0 36.8 reduce-scatter.13
  288.6 22.1 reduce-scatter.15
  342.2 20.7 reduce-scatter.17
  365.9 30.0 reduce-scatter.19
  398.4 39.7 all-gather.7
  440.8 58.0 all-gather.11
